TPU v7x, 256 devices: a whole 4x4x8 slice. The times are simulated.
256 devices in a mesh: cells: 64 (over y, z, core), members: 4 (over x).
Axes of the slice: x: 4, y: 4, z: 8, core: 2. Of those that a mesh axis runs over, the one named last changes fastest.
Arguments:
- tmax: float32 [16, 97, 262144], P('members', None, 'cells'), may hold values from -24 to 24
- threshold: int32 [262144], P('cells'), may hold values from 0 to 79
- land_mask: int32 [262144], P('cells'), may hold values from 0 to 1, as said below
- region_id: int32 [262144], P('cells'), may hold values from 0 to 45, as said below
- block_fill: int32 [2048], P('cells'), may hold values from 64 to 128
- cell_area: float32 [262144], P('cells'), may hold values from 0.1 to 1
Outputs:
- region_index: float32 [16, 92, 46], P('members')
- cell_mean: float32 [92, 262144], P('members', 'cells')
- land_count: int32 [46], replicated
Inputs may be any that keep to these rules, and one draw needn't show every extreme that they name: `land_mask`: in every block of 128 slots the first 46 slots are land. `region_id`: in every block of 128 slots the first 46 slots name every region once.
All inputs are finite; a program needn't handle non-finite values.
Results may differ from a plain program's by a relative error of at most 0.0003.
Values sent between devices are 32-bit elements; how exact they have to be, the bound alone decides.
No kernel may reach another device: no remote copies, remote signals or barrier semaphores. Data moves between devices by JAX's collectives and lax.ppermute only.
A program may use at most 64 MiB of HBM per device.

v0:
```python
import jax
import jax.numpy as jnp
from jax import lax
from jax.sharding import PartitionSpec as P

WINDOW = 6
REGIONS = 46


def filled_up(lines, length):
    spare = -lines.shape[0] % length
    if not spare:
        return lines
    return jnp.concatenate([lines, jnp.zeros((spare, *lines.shape[1:]), lines.dtype)])


def from_everyone(array, axis):
    copies = jnp.broadcast_to(array, (lax.axis_size(axis), *array.shape))
    return lax.all_to_all(copies, axis, split_axis=0, concat_axis=0, tiled=True)


def in_order(parts, dim):
    shape = list(parts.shape[1:])
    shape[dim] *= parts.shape[0]
    return jnp.moveaxis(parts, 0, dim).reshape(shape)


def collect(array, axis, dim):
    parts = from_everyone(array, axis)
    return in_order(parts, dim)


def split_up(array, dim, length):
    shape = array.shape
    parts = array.reshape(*shape[:dim], length, shape[dim] // length, *shape[dim + 1 :])
    return jnp.moveaxis(parts, dim, 0)


def sent_and_summed(array, axis, dim):
    parts = split_up(array, dim, lax.axis_size(axis))
    arrived = lax.all_to_all(parts, axis, split_axis=0, concat_axis=0, tiled=True)
    return arrived.sum(axis=0)


def sum_by_parts(array, axes):
    padded = filled_up(array, lax.axis_size(axes))
    whole = collect(sent_and_summed(padded, axes, 0), axes, 0)
    return lax.slice_in_dim(whole, 0, len(array)).reshape(array.shape)


def in_one(arrays, axis):
    ravelled, at, done = (jnp.concatenate([a.reshape(-1) for a in arrays]), 0, [])
    so_far = sum_by_parts(ravelled, axis)
    for a in arrays:
        done.append(so_far[at : at + a.size].reshape(a.shape))
        at += a.size
    return tuple(done)


def shards(tmax, threshold, land_mask, region_id, block_fill, cell_area):
    blocks = block_fill.shape[0]
    cell_dev = threshold.shape[0]
    slots = cell_dev // blocks
    position = lax.broadcasted_iota(jnp.int32, (blocks, slots), 1)
    inside = (position < block_fill[:, None]).astype(jnp.int32).reshape(cell_dev)
    live = land_mask * inside
    livef = live.astype(jnp.float32)
    weight = cell_area * livef
    matches = region_id[:, None] == jnp.arange(REGIONS, dtype=jnp.int32)[None, :]
    onehot = matches.astype(jnp.float32)
    area_part = jnp.dot(weight, onehot, precision=lax.Precision.HIGHEST)
    count_part = jnp.dot(livef, onehot, precision=lax.Precision.HIGHEST)
    limit = threshold.astype(jnp.float32) * 0.1
    members_here = tmax.shape[0]
    days = tmax.shape[1] - WINDOW + 1
    excess = jnp.maximum(tmax - limit[None, None, :], 0.0)
    rolled = excess[:, 0:days]
    for shift in range(1, WINDOW):
        rolled = rolled + excess[:, shift : shift + days]
    rolled = rolled / WINDOW
    weighted = (rolled * weight[None, None, :]).reshape(members_here * days, cell_dev)
    partial_value = jnp.dot(weighted, onehot, precision=lax.Precision.HIGHEST).reshape(
        members_here, days, REGIONS
    )
    sums, area_sum, counted = in_one((partial_value, area_part, count_part), "cells")
    region_index = sums / area_sum[None, None, :]
    land_count = counted.astype(jnp.int32)
    ensemble = lax.axis_size("members") * members_here
    member_part = jnp.sum(rolled, axis=0) * livef[None, :] / ensemble
    cell_mean = sent_and_summed(member_part, "members", 0)
    return (region_index, cell_mean, land_count)


def solution(mesh):
    return jax.shard_map(
        shards,
        mesh=mesh,
        in_specs=(
            P("members", None, "cells"),
            P("cells"),
            P("cells"),
            P("cells"),
            P("cells"),
            P("cells"),
        ),
        out_specs=(P("members", None, None), P("members", "cells"), P()),
        check_vma=False,
    )
```

profile of v0, /device:TPU:1, one launch (start us, length us, event | category | flops | bytes accessed | tf_op | source)
XLA Modules:
  0.0 102.2 jit_solution(2380541256916872866)
XLA Ops:
  0.6 0.7 convert_multiply_fusion
  1.4 4.5 %subtract_maximum_fusion = f32[4,97,4096]{2,0,1:T(4,128)S(1)} fusion(f32[4,97,4096]{2,0,1:T(4,128)} %param.6, f32[4096]{0:T(1024)S(1)} %convert_multiply_fusion), kind=kLoop, calls=%fused_computation | loop fusion | flops 3178496 | bytes 12730368 | tf_op jit(solution)/shard_map/max | solution.py:76
  5.8 0.0 copy-start.1
  5.8 0.0 copy-start.2
  5.8 0.0 copy-start.3
  5.8 12.3 %multiply_reduce_fusion = (f32[92,4096]{1,0:T(8,128)S(1)}, f32[4,92,4096]{2,0,1:T(4,128)S(1)}) fusion(f32[4,97,4096]{2,0,1:T(4,128)S(1)} %subtract_maximum_fusion), kind=kLoop, calls=%fused_computation.6 | loop fusion | flops 10174464 | bytes 43712512 | tf_op jit(solution)/shard_map/reduce_sum | solution.py:89
  18.2 0.0 copy-done.1
  18.2 0.0 copy-done.2
  18.2 0.0 copy-done.3
  18.2 0.1 broadcast_multiply_fusion.1
  18.3 1.3 %broadcast_multiply_fusion = f32[4,92,4096]{2,0,1:T(4,128)S(1)} fusion(f32[4,92,4096]{2,0,1:T(4,128)S(1)} %get-tuple-element.13, f32[4096]{0:T(1024)S(1)} %get-tuple-element.14), kind=kLoop, calls=%fused_computation.7 | loop fusion | flops 1507328 | bytes 12075008 | tf_op jit(solution)/shard_map/mul | solution.py:81
  19.7 6.1 %copy.15 = f32[4,92,4096]{2,1,0:T(8,128)} copy(f32[4,92,4096]{2,0,1:T(4,128)S(1)} %broadcast_multiply_fusion) | data formatting | bytes 12058624 | tf_op jit(solution)/shard_map/mul | solution.py:81
  25.8 0.0 copy-start
  25.8 4.8 %reshape.41 = f32[368,4096]{1,0:T(8,128)} reshape(f32[4,92,4096]{2,1,0:T(8,128)} %copy.15) | data formatting | bytes 12058624 | tf_op jit(solution)/shard_map/reshape | solution.py:81
  30.6 0.0 copy-done
  30.6 5.6 %fusion = f32[368,46]{1,0:T(8,128)S(1)} fusion(f32[368,4096]{1,0:T(8,128)} %reshape.41, s32[4096]{0:T(1024)S(1)} %copy-done), kind=kOutput, calls=%fused_computation.12 | convolution fusion | flops 832233472 | bytes 6113408 | tf_op jit(solution)/shard_map/dot_general | solution.py:82
  36.1 0.2 reshape_reshape.3
  36.3 0.5 convolution_bitcast_fusion.1
  36.8 0.5 convolution_bitcast_fusion
  37.3 0.1 concatenate.3
  37.3 0.9 all_to_all.13
  38.3 13.2 %all-to-all-start = ((f32[64,1,266]{2,1,0:T(1,128)}), f32[64,1,266]{2,1,0:T(1,128)S(1)}, u32[]{:S(2)}, u32[]{:S(2)}) async-start(f32[64,1,266]{2,1,0:T(1,128)} %all_to_all.13), calls=%async_computation | async-start | bytes 196608 | tf_op jit(solution)/shard_map/all_to_all | solution.py:41
  51.4 0.2 reduce_sum.31
  51.6 10.0 %all-to-all-done = f32[64,1,266]{2,1,0:T(1,128)S(1)} async-done(((f32[64,1,266]{2,1,0:T(1,128)}), f32[64,1,266]{2,1,0:T(1,128)S(1)}, u32[]{:S(2)}, u32[]{:S(2)}) %all-to-all-start) | async-done | bytes 68128 | tf_op jit(solution)/shard_map/all_to_all | solution.py:41
  61.6 0.1 reduce_sum.29
  61.7 0.7 broadcast_in_dim.2
  62.4 4.4 %all-to-all-start.1 = ((f32[64,1,266]{2,1,0:T(1,128)}), f32[64,1,266]{2,1,0:T(1,128)S(1)}, u32[]{:S(2)}, u32[]{:S(2)}) async-start(f32[64,1,266]{2,1,0:T(1,128)} %broadcast_in_dim.2), calls=%async_computation.1 | async-start | bytes 196608 | tf_op jit(solution)/shard_map/all_to_all | solution.py:19
  66.9 1.3 %multiply_multiply_fusion = f32[4,23,4096]{2,1,0:T(8,128)} fusion(f32[4,23,4096]{2,1,0:T(8,128)S(1)} %reduce_sum.31, f32[4096]{0:T(1024)S(1)} %get-tuple-element.16), kind=kLoop, calls=%fused_computation.8 | loop fusion | flops 753664 | bytes 3031040 | tf_op jit(solution)/shard_map/div | solution.py:89
  68.2 9.0 %all-to-all-done.1 = f32[64,1,266]{2,1,0:T(1,128)S(1)} async-done(((f32[64,1,266]{2,1,0:T(1,128)}), f32[64,1,266]{2,1,0:T(1,128)S(1)}, u32[]{:S(2)}, u32[]{:S(2)}) %all-to-all-start.1) | async-done | bytes 68128 | tf_op jit(solution)/shard_map/all_to_all | solution.py:19
  77.2 4.0 %all-to-all-start.2 = ((f32[4,23,4096]{2,1,0:T(8,128)}), f32[4,23,4096]{2,1,0:T(8,128)S(1)}, u32[]{:S(2)}, u32[]{:S(2)}) async-start(f32[4,23,4096]{2,1,0:T(8,128)} %multiply_multiply_fusion), calls=%async_computation.2 | async-start | bytes 3145728 | tf_op jit(solution)/shard_map/all_to_all | solution.py:41
  81.2 0.2 reduce.1
  81.4 0.2 reshape.42
  81.6 0.2 reshape.43
  81.8 0.6 slice_convert_fusion
  82.4 0.8 copy.18
  83.2 18.1 %all-to-all-done.2 = f32[4,23,4096]{2,1,0:T(8,128)S(1)} async-done(((f32[4,23,4096]{2,1,0:T(8,128)}), f32[4,23,4096]{2,1,0:T(8,128)S(1)}, u32[]{:S(2)}, u32[]{:S(2)}) %all-to-all-start.2) | async-done | bytes 1507360 | tf_op jit(solution)/shard_map/all_to_all | solution.py:41
  101.3 0.9 reduce_sum.32
  (2 shorter events, 0.0 us)
Async XLA Ops:
  5.8 12.4 %copy-start.1 = (f32[4096]{0:T(1024)S(1)}, f32[4096]{0:T(1024)}, u32[]{:S(2)}) copy-start(f32[4096]{0:T(1024)} %param.11) | copy-start | bytes 49156
  5.8 12.4 %copy-start.2 = (s32[4096]{0:T(1024)S(1)}, s32[4096]{0:T(1024)}, u32[]{:S(2)}) copy-start(s32[4096]{0:T(1024)} %param.8) | copy-start | bytes 49156
  5.8 12.4 %copy-start.3 = (s32[32]{0:T(128)S(1)}, s32[32]{0:T(128)}, u32[]{:S(2)}) copy-start(s32[32]{0:T(128)} %param.10) | copy-start | bytes 388
  25.8 4.8 %copy-start = (s32[4096]{0:T(1024)S(1)}, s32[4096]{0:T(1024)}, u32[]{:S(2)}) copy-start(s32[4096]{0:T(1024)} %param.9) | copy-start | bytes 49156
  38.3 23.3 %all-to-all-start = ((f32[64,1,266]{2,1,0:T(1,128)}), f32[64,1,266]{2,1,0:T(1,128)S(1)}, u32[]{:S(2)}, u32[]{:S(2)}) async-start(f32[64,1,266]{2,1,0:T(1,128)} %all_to_all.13), calls=%async_computation | async-start | bytes 196608 | tf_op jit(solution)/shard_map/all_to_all | solution.py:41
  62.4 14.7 %all-to-all-start.1 = ((f32[64,1,266]{2,1,0:T(1,128)}), f32[64,1,266]{2,1,0:T(1,128)S(1)}, u32[]{:S(2)}, u32[]{:S(2)}) async-start(f32[64,1,266]{2,1,0:T(1,128)} %broadcast_in_dim.2), calls=%async_computation.1 | async-start | bytes 196608 | tf_op jit(solution)/shard_map/all_to_all | solution.py:19
  77.2 24.1 %all-to-all-start.2 = ((f32[4,23,4096]{2,1,0:T(8,128)}), f32[4,23,4096]{2,1,0:T(8,128)S(1)}, u32[]{:S(2)}, u32[]{:S(2)}) async-start(f32[4,23,4096]{2,1,0:T(8,128)} %multiply_multiply_fusion), calls=%async_computation.2 | async-start | bytes 3145728 | tf_op jit(solution)/shard_map/all_to_all | solution.py:41
where the time goes:
time: 103 us; the launch traced here: 102 us
  waiting for transfers between devices  37.1 us (36%)
  other arithmetic  22 us (21%)
  starting transfers between devices  21.6 us (21%)
  local copies, waits for them, and re-layouts  14.1 us (14%)
  matrix products  6.5 us (6%)
    all_to_all x2, waiting for transfers between devices, sent_and_summed(): lax.all_to_all(parts, axis, split_axis=0, concat_axis=0, tiled=True)  28.1 us
    all_to_all x2, starting transfers between devices, sent_and_summed(): lax.all_to_all(parts, axis, split_axis=0, concat_axis=0, tiled=True)  17.2 us
    reduce_sum x1, other arithmetic, shards(): member_part = jnp.sum(rolled, axis=0) * livef[None, :] / ensemble  12.3 us
    all_to_all x1, waiting for transfers between devices, from_everyone(): return lax.all_to_all(copies, axis, split_axis=0, concat_axis=0, tiled=True)  9 us
    mul x1, local copies, waits for them, and re-layouts, shards(): rolled * weight[None, None, :]  6.14 us
    dot_general x1, matrix products, shards(): jnp.dot(weighted, onehot, precision=lax.Precision.HIGHEST)  5.57 us
    reshape x1, local copies, waits for them, and re-layouts, shards(): (rolled * weight[None, None, :]).reshape(members_here * days, cell_dev)  4.75 us
    max x1, other arithmetic, shards(): excess = jnp.maximum(tmax - limit[None, None, :], 0.0)  4.45 us
  transfers between devices with their start and end apart: 3, of which 3 were waited for; matrix products, arithmetic and copies ran while one was open for 3% of the time, Pallas kernels for 0%

commit v1 on v0

v1 whole, which is shorter than its diff:
```python
import jax
import jax.numpy as jnp
from jax import lax
from jax.experimental import pallas as pl
from jax.experimental.pallas import tpu as pltpu
from jax.sharding import Mesh, PartitionSpec as P

WINDOW = 6
REGIONS = 46
HALF = 64
CELL_AXES = ("y", "z", "core")


def fold_kernel(
    fill_ref, x_ref, thr_ref, mask_ref, rid_ref, area_ref,
    own_ref, up_ref, far_ref, down_ref, sums_ref, acc_ref, total_ref,
):
    step = pl.program_id(0)
    days_in = x_ref.shape[0]
    tiles = thr_ref.shape[0]
    members = x_ref.shape[1] // tiles
    block_days = own_ref.shape[0]
    lanes = thr_ref.shape[1]

    sub = lax.broadcasted_iota(jnp.int32, (tiles, lanes), 0)
    lane = lax.broadcasted_iota(jnp.int32, (tiles, lanes), 1)
    fill = jnp.zeros((tiles, lanes), jnp.int32)
    for r in range(tiles):
        fill = jnp.where(sub == r, fill_ref[step * tiles + r], fill)
    live = jnp.where(lane < fill, mask_ref[...], 0).astype(jnp.float32)
    weight = area_ref[...] * live
    limit = thr_ref[...].astype(jnp.float32) * 0.1

    total = None
    for m in range(members):
        one = jnp.maximum(x_ref[:, pl.ds(m, tiles, stride=members), :] - limit[None], 0.0)
        total = one if total is None else total + one
    total_ref[...] = total
    me = lax.axis_index("x")
    parts = 4
    scale = live * (1.0 / (WINDOW * members * parts))
    for k, out in enumerate((own_ref, up_ref, far_ref, down_ref)):
        first = lax.rem(me + k, parts) * block_days
        s = total_ref[pl.ds(first, block_days + WINDOW - 1)]
        pair = s[:-1] + s[1:]
        rolled = pair[0:block_days] + pair[2 : 2 + block_days] + pair[4 : 4 + block_days]
        out[...] = rolled * scale[None]

    group = 2 * members
    region = lax.broadcasted_iota(jnp.int32, (HALF, lanes), 0)
    part = None
    for pair in range(0, tiles // 2, 2):
        lefts, rights = [], []
        for p in (pair, pair + 1):
            def spread(v):
                rows = [jnp.broadcast_to(v[t : t + 1], (members, lanes)) for t in (2 * p, 2 * p + 1)]
                return jnp.concatenate(rows, axis=0)
            w8, l8, t8 = spread(weight), spread(live), spread(limit)
            x = x_ref[:, p * group : (p + 1) * group, :]
            e = jnp.maximum(x - t8[None], 0.0) * w8[None]
            e = e.reshape(days_in * group, lanes)
            lefts.append(jnp.concatenate([e, w8, l8], axis=0))
            hot = [
                (region == rid_ref[t : t + 1, :]).astype(jnp.float32) for t in (2 * p, 2 * p + 1)
            ]
            rights.append(jnp.concatenate(hot, axis=0))
        left = jnp.concatenate(lefts, axis=1)
        right = jnp.concatenate(rights, axis=1).astype(jnp.bfloat16)
        high = left.astype(jnp.bfloat16)
        low = (left - high.astype(jnp.float32)).astype(jnp.bfloat16)
        dims = (((1,), (1,)), ((), ()))
        both = lax.dot_general(high, right, dims, preferred_element_type=jnp.float32)
        both = both + lax.dot_general(low, right, dims, preferred_element_type=jnp.float32)
        part = both if part is None else part + both

    @pl.when(step == 0)
    def _():
        acc_ref[...] = part

    @pl.when(step > 0)
    def _():
        acc_ref[...] += part

    @pl.when(step == pl.num_programs(0) - 1)
    def _():
        days = days_in - WINDOW + 1
        v = acc_ref[...].reshape(days_in + 2, group, 2 * HALF)
        pair = v[: days_in - 1] + v[1:days_in]
        rolled = (pair[0:days] + pair[2 : 2 + days] + pair[4 : 4 + days]) * (1.0 / WINDOW)
        slots = sums_ref.shape[0]
        pad = jnp.zeros((4 * slots - days - 2, group, 2 * HALF), jnp.float32)
        v = jnp.concatenate([rolled, v[days_in:], pad], axis=0)
        s = v + pltpu.roll(pltpu.roll(v, members, 1), HALF, 2)
        r = pltpu.roll(s, HALF, 2)
        top = lax.broadcasted_iota(jnp.int32, (slots, group, 2 * HALF), 1) < members
        low = lax.broadcasted_iota(jnp.int32, (slots, group, 2 * HALF), 2) < HALF
        upper = jnp.where(low, s[0:slots], r[slots : 2 * slots])
        lower = jnp.where(low, r[2 * slots : 3 * slots], s[3 * slots :])
        sums_ref[...] = jnp.where(top, upper, lower)


def fold(x, thr, mask, rid, fill, area):
    days_in, rows, lanes = x.shape
    tiles = thr.shape[0]
    members = rows // tiles
    days = days_in - WINDOW + 1
    block_days = days // 4
    step_tiles = 8
    slots = 24
    flat = pl.BlockSpec((step_tiles, lanes), lambda i: (i, 0))
    block = jax.ShapeDtypeStruct((block_days, tiles, lanes), jnp.float32)
    return pl.pallas_call(
        fold_kernel,
        grid=(tiles // step_tiles,),
        in_specs=[
            pl.BlockSpec(memory_space=pltpu.SMEM),
            pl.BlockSpec((days_in, step_tiles * members, lanes), lambda i: (0, i, 0)),
            flat, flat, flat, flat,
        ],
        out_specs=[pl.BlockSpec((block_days, step_tiles, lanes), lambda i: (0, i, 0))] * 4
        + [pl.BlockSpec((slots, 2 * members, 2 * HALF), lambda i: (0, 0, 0))],
        out_shape=[block] * 4
        + [jax.ShapeDtypeStruct((slots, 2 * members, 2 * HALF), jnp.float32)],
        scratch_shapes=[
            pltpu.VMEM(((days_in + 2) * 2 * members, 2 * HALF), jnp.float32),
            pltpu.VMEM((days_in, step_tiles, lanes), jnp.float32),
        ],
        compiler_params=pltpu.CompilerParams(vmem_limit_bytes=40 * 1024 * 1024),
    )(fill, pltpu.with_memory_space_constraint(x, pltpu.HBM), thr, mask, rid, area)


def moved(array, axis, shift):
    size = lax.axis_size(axis)
    return lax.ppermute(array, axis, [(i, (i + shift) % size) for i in range(size)])


def sum_over_cells(sums, arrived):
    core = lax.axis_index("core")
    halves = sums.reshape(2, -1, *sums.shape[1:])
    mine = lax.dynamic_index_in_dim(halves, core, 0, False)
    other = lax.dynamic_index_in_dim(halves, 1 - core, 0, False)
    mine = mine + moved(other, "core", 1)
    mine = mine + moved(mine, "y", 1) + moved(mine, "y", 2) + moved(mine, "y", 3)
    above, below = moved(mine, "z", 7), moved(mine, "z", 1)
    two = mine + above
    three = two + below
    mine = three + moved(three, "z", 5) + moved(two, "z", 3)
    mine, arrived = lax.optimization_barrier((mine, arrived))
    other = moved(mine, "core", 1)
    first = jnp.where(core == 0, mine, other)
    second = jnp.where(core == 0, other, mine)
    return jnp.concatenate([first, second]), arrived


def shards(tmax, threshold, land_mask, region_id, block_fill, cell_area):
    members, days_in, cells = tmax.shape
    blocks = block_fill.shape[0]
    lanes = cells // blocks
    days = days_in - WINDOW + 1
    x = tmax.reshape(members, days_in, blocks, lanes).transpose(1, 2, 0, 3)
    x = x.reshape(days_in, blocks * members, lanes)
    tile = lambda a: a.reshape(blocks, lanes)
    own, up, far, down, sums = fold(
        x, tile(threshold), tile(land_mask), tile(region_id), block_fill, tile(cell_area)
    )
    arrived = (moved(up, "x", 1), moved(far, "x", 2), moved(down, "x", 3))
    sums, arrived = sum_over_cells(sums, arrived)
    cell_mean = (own + arrived[0] + arrived[1] + arrived[2]).reshape(-1, cells)
    slots = sums.shape[0]
    table = sums.reshape(slots, 2, members, 2, HALF).transpose(2, 1, 3, 0, 4)
    table = table.reshape(members, 4 * slots, HALF)[:, :, :REGIONS]
    region_index = table[:, :days] / table[:, days : days + 1]
    land_count = table[0, days + 1].astype(jnp.int32)
    return region_index, cell_mean, land_count


def solution(mesh):
    devices = mesh.devices.reshape(4, 8, 2, 4)
    fine = Mesh(devices, ("y", "z", "core", "x"))
    cells = P(CELL_AXES)
    return jax.shard_map(
        shards,
        mesh=fine,
        in_specs=(P("x", None, CELL_AXES), cells, cells, cells, cells, cells),
        out_specs=(P("x", None, None), P("x", CELL_AXES), P()),
        check_vma=False,
    )
```

time: 103 us -> 51.7 us (0.50)
  waiting for transfers between devices: 37.1 us -> 14.9 us
  other arithmetic: 22 us -> 0.74 us
  local copies, waits for them, and re-layouts: 14.1 us -> 5.53 us
  Pallas kernels: 0 us -> 6.86 us
  matrix products: 6.5 us -> 0 us
    all_to_all x3 -> x0, waiting for transfers between devices: 37.1 us -> none  [the longest x2 28.1 us: sent_and_summed(): lax.all_to_all(parts, axis, split_axis=0, concat_axis=0, tiled=True)]
    ppermute x0 -> x12, starting transfers between devices: none -> 22.4 us  [moved(): lax.ppermute(array, axis, [(i, (i + shift) % size) for i in range(size)])]
    all_to_all x3 -> x0, starting transfers between devices: 21.6 us -> none  [the longest x2 17.2 us: sent_and_summed(): lax.all_to_all(parts, axis, split_axis=0, concat_axis=0, tiled=True)]
    ppermute x0 -> x12, waiting for transfers between devices: none -> 14.9 us  [moved(): lax.ppermute(array, axis, [(i, (i + shift) % size) for i in range(size)])]
    reduce_sum x3 -> x0, other arithmetic: 13.3 us -> none  [the longest x1 12.3 us: shards(): member_part = jnp.sum(rolled, axis=0) * livef[None, :] / ensemble]
    pallas_call x0 -> x1, Pallas kernels: none -> 6.86 us  [fold(): pl.pallas_call(fold_kernel, grid=(tiles // step_tiles,), in_specs=[pl.Blo...]
    dot_general x3 -> x0, matrix products: 6.5 us -> none  [the longest x1 5.57 us: shards(): jnp.dot(weighted, onehot, precision=lax.Precision.HIGHEST)]
    mul x1 -> x0, local copies, waits for them, and re-layouts: 6.14 us -> none  [shards(): rolled * weight[None, None, :]]
  transfers between devices with their start and end apart: 3 -> 12, of which waited for: 3 -> 7; matrix products, arithmetic and copies ran while one was open for 3% -> 2% of each run, Pallas kernels for 0% -> 0%
where the time goes in v1:
time: 51.7 us; the launch traced here: 51.2 us
  starting transfers between devices  22.4 us (43%)
  waiting for transfers between devices  14.9 us (29%)
  Pallas kernels  6.86 us (13%)
  local copies, waits for them, and re-layouts  5.53 us (11%)
  other arithmetic  0.74 us (1%)
  between operations  0.74 us (1%)
    ppermute x12, starting transfers between devices, moved(): lax.ppermute(array, axis, [(i, (i + shift) % size) for i in range(size)])  22.4 us
    ppermute x12, waiting for transfers between devices, moved(): lax.ppermute(array, axis, [(i, (i + shift) % size) for i in range(size)])  14.9 us
    pallas_call x1, Pallas kernels, fold(): pl.pallas_call(fold_kernel, grid=(tiles // step_tiles,), in_specs=[pl.Blo...  6.86 us
    unnamed x13, local copies, waits for them, and re-layouts  5.29 us
  transfers between devices with their start and end apart: 12, of which 7 were waited for; matrix products, arithmetic and copies ran while one was open for 2% of the time, Pallas kernels for 0%

profile of v1, /device:TPU:1, one launch (start us, length us, event | category | flops | bytes accessed | tf_op | source)
XLA Modules:
  0.0 51.2 jit_solution(4623067162809050082)
XLA Ops:
  0.6 0.0 copy-start
  0.6 0.7 %copy-done = s32[4096]{0:T(1024)S(1)} copy-done((s32[4096]{0:T(1024)S(1)}, s32[4096]{0:T(1024)}, u32[]{:S(2)}) %copy-start) | copy-done | bytes 16408
  1.4 0.0 copy-start.1
  1.4 0.7 %copy-done.1 = s32[4096]{0:T(1024)S(1)} copy-done((s32[4096]{0:T(1024)S(1)}, s32[4096]{0:T(1024)}, u32[]{:S(2)}) %copy-start.1) | copy-done | bytes 16408
  2.1 0.0 copy-start.2
  2.1 0.7 %copy-done.2 = s32[4096]{0:T(1024)S(1)} copy-done((s32[4096]{0:T(1024)S(1)}, s32[4096]{0:T(1024)}, u32[]{:S(2)}) %copy-start.2) | copy-done | bytes 16408
  2.8 0.0 copy-start.3
  2.8 0.7 %copy-done.3 = f32[4096]{0:T(1024)S(1)} copy-done((f32[4096]{0:T(1024)S(1)}, f32[4096]{0:T(1024)}, u32[]{:S(2)}) %copy-start.3) | copy-done | bytes 16408
  3.5 0.0 copy-start.4
  3.5 0.7 %copy-done.4 = s32[32]{0:T(128)S(1)} copy-done((s32[32]{0:T(128)S(1)}, s32[32]{0:T(128)}, u32[]{:S(2)}) %copy-start.4) | copy-done | bytes 152
  4.2 6.9 %shard_map.85 = (f32[23,32,128]{2,1,0:T(8,128)S(1)}, f32[23,32,128]{2,1,0:T(8,128)S(1)}, f32[23,32,128]{2,1,0:T(8,128)S(1)}, f32[23,32,128]{2,1,0:T(8,128)S(1)}, f32[24,8,128]{2,1,0:T(8,128)S(1)}) custom-call(s32[32]{0:T(128)S(1)} %copy-done.4, f32[97,128,128]{2,1,0:T(8,128)} %bitcast.28, s32[32,128]{1,0:T(8,128)S(1)} %bitcast.24, s32[32,128]{1,0:T(8,128)S(1)} %bitcast.25, ...), custom_call_target="tpu_custom_call" | custom-call | tf_op jit(solution)/shard_map/pallas_call | solution.py:112
  11.1 3.3 %collective-permute-start = (f32[12,8,128]{2,1,0:T(8,128)S(1)}, f32[12,8,128]{2,1,0:T(8,128)S(1)}, u32[]{:S(2)}, u32[]{:S(2)}) collective-permute-start(f32[12,8,128]{2,1,0:T(8,128)S(1)} %dynamic-slice_bitcast_fusion), channel_id=1, source_target_pairs={{0,4},{4,0},{1,5},{5,1},{2,6},{6,2},{3,7},{7,3},{8,12},{12,8},{9,1... | collective-permute-start | bytes 147464 | tf_op jit(solution)/shard_map/ppermute | solution.py:134
  14.4 0.9 %collective-permute-done = f32[12,8,128]{2,1,0:T(8,128)S(1)} collective-permute-done((f32[12,8,128]{2,1,0:T(8,128)S(1)}, f32[12,8,128]{2,1,0:T(8,128)S(1)}, u32[]{:S(2)}, u32[]{:S(2)}) %collective-permute-start) | collective-permute-done | bytes 49184 | tf_op jit(solution)/shard_map/ppermute | solution.py:134
  15.3 1.0 %collective-permute-start.3 = (f32[12,8,128]{2,1,0:T(8,128)S(1)}, f32[12,8,128]{2,1,0:T(8,128)S(1)}, u32[]{:S(2)}, u32[]{:S(2)}) collective-permute-start(f32[12,8,128]{2,1,0:T(8,128)S(1)} %bitcast_add_fusion), channel_id=1, source_target_pairs={{0,192},{64,0},{128,64},{192,128},{1,193},{65,1},{129,65},{193,129... | collective-permute-start | bytes 147464 | tf_op jit(solution)/shard_map/ppermute | solution.py:134
  16.3 0.3 collective-permute-start.2
  16.7 0.7 %collective-permute-start.1 = (f32[12,8,128]{2,1,0:T(8,128)S(1)}, f32[12,8,128]{2,1,0:T(8,128)S(1)}, u32[]{:S(2)}, u32[]{:S(2)}) collective-permute-start(f32[12,8,128]{2,1,0:T(8,128)S(1)} %bitcast_add_fusion), channel_id=1, source_target_pairs={{0,64},{64,128},{128,192},{192,0},{1,65},{65,129},{129,193},{193,1... | collective-permute-start | bytes 147464 | tf_op jit(solution)/shard_map/ppermute | solution.py:134
  17.3 0.9 %collective-permute-done.3 = f32[12,8,128]{2,1,0:T(8,128)S(1)} collective-permute-done((f32[12,8,128]{2,1,0:T(8,128)S(1)}, f32[12,8,128]{2,1,0:T(8,128)S(1)}, u32[]{:S(2)}, u32[]{:S(2)}) %collective-permute-start.3) | collective-permute-done | bytes 49184 | tf_op jit(solution)/shard_map/ppermute | solution.py:134
  18.2 2.6 %collective-permute-done.2 = f32[12,8,128]{2,1,0:T(8,128)S(1)} collective-permute-done((f32[12,8,128]{2,1,0:T(8,128)S(1)}, f32[12,8,128]{2,1,0:T(8,128)S(1)}, u32[]{:S(2)}, u32[]{:S(2)}) %collective-permute-start.2) | collective-permute-done | bytes 49184 | tf_op jit(solution)/shard_map/ppermute | solution.py:134
  20.8 0.5 collective-permute-done.1
  21.3 1.7 %collective-permute-start.5 = (f32[12,8,128]{2,1,0:T(8,128)S(1)}, f32[12,8,128]{2,1,0:T(8,128)S(1)}, u32[]{:S(2)}, u32[]{:S(2)}) collective-permute-start(f32[12,8,128]{2,1,0:T(8,128)S(1)} %add_add_fusion.2), channel_id=1, source_target_pairs={{0,8},{8,16},{16,24},{24,32},{32,40},{40,48},{48,56},{56,0},{1,9},... | collective-permute-start | bytes 147464 | tf_op jit(solution)/shard_map/ppermute | solution.py:134
  23.0 4.0 %collective-permute-start.4 = (f32[12,8,128]{2,1,0:T(8,128)S(1)}, f32[12,8,128]{2,1,0:T(8,128)S(1)}, u32[]{:S(2)}, u32[]{:S(2)}) collective-permute-start(f32[12,8,128]{2,1,0:T(8,128)S(1)} %add_add_fusion.2), channel_id=1, source_target_pairs={{0,56},{8,0},{16,8},{24,16},{32,24},{40,32},{48,40},{56,48},{1,57}... | collective-permute-start | bytes 147464 | tf_op jit(solution)/shard_map/ppermute | solution.py:134
  27.0 1.2 %collective-permute-start.8 = (f32[23,32,128]{2,1,0:T(8,128)S(1)}, f32[23,32,128]{2,1,0:T(8,128)S(1)}, u32[]{:S(2)}, u32[]{:S(2)}) collective-permute-start(f32[23,32,128]{2,1,0:T(8,128)S(1)} %get-tuple-element.13), channel_id=1, source_target_pairs={{0,1},{1,2},{2,3},{3,0},{4,5},{5,6},{6,7},{7,4},{8,9},{9,10},{10,1... | collective-permute-start | bytes 1130504 | tf_op jit(solution)/shard_map/ppermute | solution.py:134
  28.2 2.5 %collective-permute-start.9 = (f32[23,32,128]{2,1,0:T(8,128)S(1)}, f32[23,32,128]{2,1,0:T(8,128)S(1)}, u32[]{:S(2)}, u32[]{:S(2)}) collective-permute-start(f32[23,32,128]{2,1,0:T(8,128)S(1)} %get-tuple-element.14), channel_id=1, source_target_pairs={{0,2},{1,3},{2,0},{3,1},{4,6},{5,7},{6,4},{7,5},{8,10},{9,11},{10,... | collective-permute-start | bytes 1130504 | tf_op jit(solution)/shard_map/ppermute | solution.py:134
  30.7 1.2 %collective-permute-start.10 = (f32[23,32,128]{2,1,0:T(8,128)S(1)}, f32[23,32,128]{2,1,0:T(8,128)S(1)}, u32[]{:S(2)}, u32[]{:S(2)}) collective-permute-start(f32[23,32,128]{2,1,0:T(8,128)S(1)} %get-tuple-element.15), channel_id=1, source_target_pairs={{0,3},{1,0},{2,1},{3,2},{4,7},{5,4},{6,5},{7,6},{8,11},{9,8},{10,9... | collective-permute-start | bytes 1130504 | tf_op jit(solution)/shard_map/ppermute | solution.py:134
  31.8 0.0 collective-permute-done.5
  31.9 0.0 collective-permute-done.4
  31.9 1.6 %collective-permute-start.7 = (f32[12,8,128]{2,1,0:T(8,128)S(1)}, f32[12,8,128]{2,1,0:T(8,128)S(1)}, u32[]{:S(2)}, u32[]{:S(2)}) collective-permute-start(f32[12,8,128]{2,1,0:T(8,128)S(1)} %get-tuple-element.25), channel_id=1, source_target_pairs={{0,24},{8,32},{16,40},{24,48},{32,56},{40,0},{48,8},{56,16},{1,25}... | collective-permute-start | bytes 147464 | tf_op jit(solution)/shard_map/ppermute | solution.py:134
  33.5 2.9 %collective-permute-start.6 = (f32[12,8,128]{2,1,0:T(8,128)S(1)}, f32[12,8,128]{2,1,0:T(8,128)S(1)}, u32[]{:S(2)}, u32[]{:S(2)}) collective-permute-start(f32[12,8,128]{2,1,0:T(8,128)S(1)} %get-tuple-element.24), channel_id=1, source_target_pairs={{0,40},{8,48},{16,56},{24,0},{32,8},{40,16},{48,24},{56,32},{1,41}... | collective-permute-start | bytes 147464 | tf_op jit(solution)/shard_map/ppermute | solution.py:134
  36.4 2.0 %collective-permute-done.7 = f32[12,8,128]{2,1,0:T(8,128)S(1)} collective-permute-done((f32[12,8,128]{2,1,0:T(8,128)S(1)}, f32[12,8,128]{2,1,0:T(8,128)S(1)}, u32[]{:S(2)}, u32[]{:S(2)}) %collective-permute-start.7) | collective-permute-done | bytes 49184 | tf_op jit(solution)/shard_map/ppermute | solution.py:134
  38.4 0.0 collective-permute-done.6
  38.4 0.0 collective-permute-done.8
  38.5 7.0 %collective-permute-done.9 = f32[23,32,128]{2,1,0:T(8,128)S(1)} collective-permute-done((f32[23,32,128]{2,1,0:T(8,128)S(1)}, f32[23,32,128]{2,1,0:T(8,128)S(1)}, u32[]{:S(2)}, u32[]{:S(2)}) %collective-permute-start.9) | collective-permute-done | bytes 376864 | tf_op jit(solution)/shard_map/ppermute | solution.py:134
  45.5 1.1 %collective-permute-done.10 = f32[23,32,128]{2,1,0:T(8,128)S(1)} collective-permute-done((f32[23,32,128]{2,1,0:T(8,128)S(1)}, f32[23,32,128]{2,1,0:T(8,128)S(1)}, u32[]{:S(2)}, u32[]{:S(2)}) %collective-permute-start.10) | collective-permute-done | bytes 376864 | tf_op jit(solution)/shard_map/ppermute | solution.py:134
  46.6 1.9 %collective-permute-start.11 = (f32[12,8,128]{2,1,0:T(8,128)S(1)}, f32[12,8,128]{2,1,0:T(8,128)S(1)}, u32[]{:S(2)}, u32[]{:S(2)}) collective-permute-start(f32[12,8,128]{2,1,0:T(8,128)S(1)} %add_add_fusion.1), channel_id=1, source_target_pairs={{0,4},{4,0},{1,5},{5,1},{2,6},{6,2},{3,7},{7,3},{8,12},{12,8},{9,1... | collective-permute-start | bytes 147464 | tf_op jit(solution)/shard_map/ppermute | solution.py:134
  48.5 0.1 add_add_fusion
  48.7 1.0 %copy.13 = f32[3,8,32,128]{3,1,2,0:T(8,128)} copy(f32[3,8,32,128]{3,2,1,0:T(8,128)S(1)} %bitcast.29) | data formatting | bytes 786432
  49.6 0.0 collective-permute-done.11
  49.7 0.2 reshape.44
  49.8 0.1 copy.11
  49.9 0.5 %fusion = s32[46]{0:T(128)} fusion(f32[4,96,64]{2,1,0:T(8,128)S(1)} %bitcast.30), kind=kLoop, calls=%fused_computation.10 | loop fusion | flops 46 | bytes 368 | tf_op jit(solution)/shard_map/convert_element_type | solution.py:173
  50.5 0.8 %copy.12 = f32[4,92,46]{1,0,2:T(4,128)} copy(f32[4,92,46]{2,1,0:T(8,128)S(1)} %slice_divide_fusion) | data formatting | bytes 135424
  (10 shorter events, 0.1 us)
Async XLA Ops:
  0.6 0.7 %copy-start = (s32[4096]{0:T(1024)S(1)}, s32[4096]{0:T(1024)}, u32[]{:S(2)}) copy-start(s32[4096]{0:T(1024)} %param.7) | copy-start | bytes 49156
  1.4 0.7 %copy-start.1 = (s32[4096]{0:T(1024)S(1)}, s32[4096]{0:T(1024)}, u32[]{:S(2)}) copy-start(s32[4096]{0:T(1024)} %param.8) | copy-start | bytes 49156
  2.1 0.7 %copy-start.2 = (s32[4096]{0:T(1024)S(1)}, s32[4096]{0:T(1024)}, u32[]{:S(2)}) copy-start(s32[4096]{0:T(1024)} %param.9) | copy-start | bytes 49156
  2.8 0.7 %copy-start.3 = (f32[4096]{0:T(1024)S(1)}, f32[4096]{0:T(1024)}, u32[]{:S(2)}) copy-start(f32[4096]{0:T(1024)} %param.11) | copy-start | bytes 49156
  3.5 0.7 %copy-start.4 = (s32[32]{0:T(128)S(1)}, s32[32]{0:T(128)}, u32[]{:S(2)}) copy-start(s32[32]{0:T(128)} %fill_ref.1) | copy-start | bytes 388
  11.1 4.2 %collective-permute-start = (f32[12,8,128]{2,1,0:T(8,128)S(1)}, f32[12,8,128]{2,1,0:T(8,128)S(1)}, u32[]{:S(2)}, u32[]{:S(2)}) collective-permute-start(f32[12,8,128]{2,1,0:T(8,128)S(1)} %dynamic-slice_bitcast_fusion), channel_id=1, source_target_pairs={{0,4},{4,0},{1,5},{5,1},{2,6},{6,2},{3,7},{7,3},{8,12},{12,8},{9,1... | collective-permute-start | bytes 147464 | tf_op jit(solution)/shard_map/ppermute | solution.py:134
  15.3 3.0 %collective-permute-start.3 = (f32[12,8,128]{2,1,0:T(8,128)S(1)}, f32[12,8,128]{2,1,0:T(8,128)S(1)}, u32[]{:S(2)}, u32[]{:S(2)}) collective-permute-start(f32[12,8,128]{2,1,0:T(8,128)S(1)} %bitcast_add_fusion), channel_id=1, source_target_pairs={{0,192},{64,0},{128,64},{192,128},{1,193},{65,1},{129,65},{193,129... | collective-permute-start | bytes 147464 | tf_op jit(solution)/shard_map/ppermute | solution.py:134
  16.3 4.5 %collective-permute-start.2 = (f32[12,8,128]{2,1,0:T(8,128)S(1)}, f32[12,8,128]{2,1,0:T(8,128)S(1)}, u32[]{:S(2)}, u32[]{:S(2)}) collective-permute-start(f32[12,8,128]{2,1,0:T(8,128)S(1)} %bitcast_add_fusion), channel_id=1, source_target_pairs={{0,128},{64,192},{128,0},{192,64},{1,129},{65,193},{129,1},{193,65... | collective-permute-start | bytes 147464 | tf_op jit(solution)/shard_map/ppermute | solution.py:134
  16.7 4.6 %collective-permute-start.1 = (f32[12,8,128]{2,1,0:T(8,128)S(1)}, f32[12,8,128]{2,1,0:T(8,128)S(1)}, u32[]{:S(2)}, u32[]{:S(2)}) collective-permute-start(f32[12,8,128]{2,1,0:T(8,128)S(1)} %bitcast_add_fusion), channel_id=1, source_target_pairs={{0,64},{64,128},{128,192},{192,0},{1,65},{65,129},{129,193},{193,1... | collective-permute-start | bytes 147464 | tf_op jit(solution)/shard_map/ppermute | solution.py:134
  21.3 10.6 %collective-permute-start.5 = (f32[12,8,128]{2,1,0:T(8,128)S(1)}, f32[12,8,128]{2,1,0:T(8,128)S(1)}, u32[]{:S(2)}, u32[]{:S(2)}) collective-permute-start(f32[12,8,128]{2,1,0:T(8,128)S(1)} %add_add_fusion.2), channel_id=1, source_target_pairs={{0,8},{8,16},{16,24},{24,32},{32,40},{40,48},{48,56},{56,0},{1,9},... | collective-permute-start | bytes 147464 | tf_op jit(solution)/shard_map/ppermute | solution.py:134
  23.0 8.8 %collective-permute-start.4 = (f32[12,8,128]{2,1,0:T(8,128)S(1)}, f32[12,8,128]{2,1,0:T(8,128)S(1)}, u32[]{:S(2)}, u32[]{:S(2)}) collective-permute-start(f32[12,8,128]{2,1,0:T(8,128)S(1)} %add_add_fusion.2), channel_id=1, source_target_pairs={{0,56},{8,0},{16,8},{24,16},{32,24},{40,32},{48,40},{56,48},{1,57}... | collective-permute-start | bytes 147464 | tf_op jit(solution)/shard_map/ppermute | solution.py:134
  27.0 11.4 %collective-permute-start.8 = (f32[23,32,128]{2,1,0:T(8,128)S(1)}, f32[23,32,128]{2,1,0:T(8,128)S(1)}, u32[]{:S(2)}, u32[]{:S(2)}) collective-permute-start(f32[23,32,128]{2,1,0:T(8,128)S(1)} %get-tuple-element.13), channel_id=1, source_target_pairs={{0,1},{1,2},{2,3},{3,0},{4,5},{5,6},{6,7},{7,4},{8,9},{9,10},{10,1... | collective-permute-start | bytes 1130504 | tf_op jit(solution)/shard_map/ppermute | solution.py:134
  28.2 17.2 %collective-permute-start.9 = (f32[23,32,128]{2,1,0:T(8,128)S(1)}, f32[23,32,128]{2,1,0:T(8,128)S(1)}, u32[]{:S(2)}, u32[]{:S(2)}) collective-permute-start(f32[23,32,128]{2,1,0:T(8,128)S(1)} %get-tuple-element.14), channel_id=1, source_target_pairs={{0,2},{1,3},{2,0},{3,1},{4,6},{5,7},{6,4},{7,5},{8,10},{9,11},{10,... | collective-permute-start | bytes 1130504 | tf_op jit(solution)/shard_map/ppermute | solution.py:134
  30.7 15.9 %collective-permute-start.10 = (f32[23,32,128]{2,1,0:T(8,128)S(1)}, f32[23,32,128]{2,1,0:T(8,128)S(1)}, u32[]{:S(2)}, u32[]{:S(2)}) collective-permute-start(f32[23,32,128]{2,1,0:T(8,128)S(1)} %get-tuple-element.15), channel_id=1, source_target_pairs={{0,3},{1,0},{2,1},{3,2},{4,7},{5,4},{6,5},{7,6},{8,11},{9,8},{10,9... | collective-permute-start | bytes 1130504 | tf_op jit(solution)/shard_map/ppermute | solution.py:134
  31.9 6.6 %collective-permute-start.7 = (f32[12,8,128]{2,1,0:T(8,128)S(1)}, f32[12,8,128]{2,1,0:T(8,128)S(1)}, u32[]{:S(2)}, u32[]{:S(2)}) collective-permute-start(f32[12,8,128]{2,1,0:T(8,128)S(1)} %get-tuple-element.25), channel_id=1, source_target_pairs={{0,24},{8,32},{16,40},{24,48},{32,56},{40,0},{48,8},{56,16},{1,25}... | collective-permute-start | bytes 147464 | tf_op jit(solution)/shard_map/ppermute | solution.py:134
  33.5 4.9 %collective-permute-start.6 = (f32[12,8,128]{2,1,0:T(8,128)S(1)}, f32[12,8,128]{2,1,0:T(8,128)S(1)}, u32[]{:S(2)}, u32[]{:S(2)}) collective-permute-start(f32[12,8,128]{2,1,0:T(8,128)S(1)} %get-tuple-element.24), channel_id=1, source_target_pairs={{0,40},{8,48},{16,56},{24,0},{32,8},{40,16},{48,24},{56,32},{1,41}... | collective-permute-start | bytes 147464 | tf_op jit(solution)/shard_map/ppermute | solution.py:134
  46.6 3.1 %collective-permute-start.11 = (f32[12,8,128]{2,1,0:T(8,128)S(1)}, f32[12,8,128]{2,1,0:T(8,128)S(1)}, u32[]{:S(2)}, u32[]{:S(2)}) collective-permute-start(f32[12,8,128]{2,1,0:T(8,128)S(1)} %add_add_fusion.1), channel_id=1, source_target_pairs={{0,4},{4,0},{1,5},{5,1},{2,6},{6,2},{3,7},{7,3},{8,12},{12,8},{9,1... | collective-permute-start | bytes 147464 | tf_op jit(solution)/shard_map/ppermute | solution.py:134

commit v2 on v1

v2 whole, which is shorter than its diff:
```python
import jax
import jax.numpy as jnp
from jax import lax
from jax.experimental import pallas as pl
from jax.experimental.pallas import tpu as pltpu
from jax.sharding import Mesh, PartitionSpec as P

WINDOW = 6
REGIONS = 46
HALF = 64
PARTS = 4
SLOTS = 24
TILES = 8
CELL_AXES = ("y", "z", "core")


def live_cells(fill_ref, mask_ref, step):
    tiles, lanes = mask_ref.shape
    sub = lax.broadcasted_iota(jnp.int32, (tiles, lanes), 0)
    lane = lax.broadcasted_iota(jnp.int32, (tiles, lanes), 1)
    fill = jnp.zeros((tiles, lanes), jnp.int32)
    for r in range(tiles):
        fill = jnp.where(sub == r, fill_ref[step * tiles + r], fill)
    return jnp.where(lane < fill, mask_ref[...], 0).astype(jnp.float32)


def cell_sums(step, x_ref, live, limit, outs, total_ref):
    tiles, lanes = live.shape
    members = x_ref.shape[1] // tiles
    block_days = outs[0].shape[0]
    total = None
    for m in range(members):
        one = jnp.maximum(x_ref[:, pl.ds(m, tiles, stride=members), :] - limit[None], 0.0)
        total = one if total is None else total + one
    total_ref[...] = total
    me = lax.axis_index("x")
    scale = live * (1.0 / (WINDOW * members * PARTS))
    early = (2 * step < pl.num_programs(0)).astype(jnp.int32)
    ahead = (0, 1 + early, 2 + early, 3 - 2 * early)
    for k, out in zip(ahead, outs):
        first = lax.rem(me + k, PARTS) * block_days
        s = total_ref[pl.ds(first, block_days + WINDOW - 1)]
        pair = s[:-1] + s[1:]
        rolled = pair[0:block_days] + pair[2 : 2 + block_days] + pair[4 : 4 + block_days]
        out[...] = rolled * scale[None]


def region_sums(step, x_ref, live, weight, limit, rid_ref, sums_ref, acc_ref):
    days_in = x_ref.shape[0]
    tiles, lanes = live.shape
    members = x_ref.shape[1] // tiles
    group = 2 * members
    region = lax.broadcasted_iota(jnp.int32, (HALF, lanes), 0)

    def spread(v, t):
        rows = [jnp.broadcast_to(v[r : r + 1], (members, lanes)) for r in (t, t + 1)]
        return jnp.concatenate(rows, axis=0)

    part = None
    for pair in range(0, tiles // 2, 2):
        lefts, rights = [], []
        for p in (pair, pair + 1):
            w8, l8, t8 = spread(weight, 2 * p), spread(live, 2 * p), spread(limit, 2 * p)
            x = x_ref[:, p * group : (p + 1) * group, :]
            e = jnp.maximum(x - t8[None], 0.0) * w8[None]
            e = e.reshape(days_in * group, lanes)
            lefts.append(jnp.concatenate([e, w8, l8], axis=0))
            hot = [
                (region == rid_ref[t : t + 1, :]).astype(jnp.float32) for t in (2 * p, 2 * p + 1)
            ]
            rights.append(jnp.concatenate(hot, axis=0))
        left = jnp.concatenate(lefts, axis=1)
        right = jnp.concatenate(rights, axis=1).astype(jnp.bfloat16)
        high = left.astype(jnp.bfloat16)
        low = (left - high.astype(jnp.float32)).astype(jnp.bfloat16)
        dims = (((1,), (1,)), ((), ()))
        both = lax.dot_general(high, right, dims, preferred_element_type=jnp.float32)
        both = both + lax.dot_general(low, right, dims, preferred_element_type=jnp.float32)
        part = both if part is None else part + both

    @pl.when(step == 0)
    def _():
        acc_ref[...] = part

    @pl.when(step > 0)
    def _():
        acc_ref[...] += part

    @pl.when(step == pl.num_programs(0) - 1)
    def _():
        days = days_in - WINDOW + 1
        v = acc_ref[...].reshape(days_in + 2, group, 2 * HALF)
        pair = v[: days_in - 1] + v[1:days_in]
        rolled = (pair[0:days] + pair[2 : 2 + days] + pair[4 : 4 + days]) * (1.0 / WINDOW)
        pad = jnp.zeros((4 * SLOTS - days - 2, group, 2 * HALF), jnp.float32)
        v = jnp.concatenate([rolled, v[days_in:], pad], axis=0)
        s = v + pltpu.roll(pltpu.roll(v, members, 1), HALF, 2)
        r = pltpu.roll(s, HALF, 2)
        top = lax.broadcasted_iota(jnp.int32, (SLOTS, group, 2 * HALF), 1) < members
        low = lax.broadcasted_iota(jnp.int32, (SLOTS, group, 2 * HALF), 2) < HALF
        upper = jnp.where(low, s[0:SLOTS], r[SLOTS : 2 * SLOTS])
        lower = jnp.where(low, r[2 * SLOTS : 3 * SLOTS], s[3 * SLOTS :])
        sums_ref[...] = jnp.where(top, upper, lower)


def fold_kernel(fill_ref, x_ref, thr_ref, mask_ref, rid_ref, area_ref, *refs):
    *outs, sums_ref, acc_ref, total_ref = refs
    step = pl.program_id(0)
    live = live_cells(fill_ref, mask_ref, step)
    limit = thr_ref[...].astype(jnp.float32) * 0.1
    cell_sums(step, x_ref, live, limit, outs, total_ref)
    region_sums(step, x_ref, live, area_ref[...] * live, limit, rid_ref, sums_ref, acc_ref)


def table_kernel(mine_ref, other_ref, index_ref, count_ref, rows_ref):
    half, group, lanes = mine_ref.shape
    members = group // 2
    days = index_ref.shape[2]
    core = lax.axis_index("core")
    mine = mine_ref[...].reshape(half * group, lanes)
    other = other_ref[...].reshape(half * group, lanes)
    rows_ref[: half * group] = jnp.where(core == 0, mine, other)
    rows_ref[half * group :] = jnp.where(core == 0, other, mine)
    for m in range(members):
        upper = rows_ref[pl.ds(m, 2 * half, stride=group), :]
        lower = rows_ref[pl.ds(members + m, 2 * half, stride=group), :]
        rows = [upper, pltpu.roll(upper, HALF, 1), lower, pltpu.roll(lower, HALF, 1)]
        table = jnp.concatenate(rows, axis=0)
        if m == 0:
            count_ref[...] = table[days + 1 : days + 2, :REGIONS].astype(jnp.int32)
        by_region = table.T[:REGIONS]
        index_ref[:, m, :] = by_region[:, :days] / by_region[:, days : days + 1]


def call(kernel, fill, x, flats, blocks, regional):
    days_in, rows, lanes = x.shape
    tiles = flats[0].shape[0]
    members = rows // tiles
    block_days = (days_in - WINDOW + 1) // PARTS
    flat = pl.BlockSpec((TILES, lanes), lambda i: (i, 0))
    out_specs = [pl.BlockSpec((block_days, TILES, lanes), lambda i: (0, i, 0))] * blocks
    out_shape = [jax.ShapeDtypeStruct((block_days, tiles, lanes), jnp.float32)] * blocks
    scratch = []
    if regional:
        sums = (SLOTS, 2 * members, 2 * HALF)
        out_specs.append(pl.BlockSpec(sums, lambda i: (0, 0, 0)))
        out_shape.append(jax.ShapeDtypeStruct(sums, jnp.float32))
        scratch.append(pltpu.VMEM(((days_in + 2) * 2 * members, 2 * HALF), jnp.float32))
    if blocks:
        scratch.append(pltpu.VMEM((days_in, TILES, lanes), jnp.float32))
    return pl.pallas_call(
        kernel,
        grid=(tiles // TILES,),
        in_specs=[
            pl.BlockSpec(memory_space=pltpu.SMEM),
            pl.BlockSpec((days_in, TILES * members, lanes), lambda i: (0, i, 0)),
        ]
        + [flat] * len(flats),
        out_specs=out_specs,
        out_shape=out_shape,
        scratch_shapes=scratch,
        compiler_params=pltpu.CompilerParams(vmem_limit_bytes=40 * 1024 * 1024),
    )(*[pltpu.with_memory_space_constraint(a, pltpu.HBM) if a is not fill else a for a in (fill, x, *flats)])


def moved(array, axis, shift):
    size = lax.axis_size(axis)
    return lax.ppermute(array, axis, [(i, (i + shift) % size) for i in range(size)])


def sum_over_cells(sums):
    core = lax.axis_index("core")
    halves = sums.reshape(2, -1, *sums.shape[1:])
    mine = lax.dynamic_index_in_dim(halves, core, 0, False)
    other = lax.dynamic_index_in_dim(halves, 1 - core, 0, False)
    mine = mine + moved(other, "core", 1)
    mine = mine + moved(mine, "y", 1) + moved(mine, "y", 2) + moved(mine, "y", 3)
    two = mine + moved(mine, "z", 7)
    three = two + moved(mine, "z", 1)
    mine = three + moved(three, "z", 5) + moved(two, "z", 3)
    return mine, moved(mine, "core", 1)


def sum_over_members(own, up, down, late):
    tiles = own.shape[1]
    cut = tiles // 2
    from_below, from_above = moved(up, "x", 1), moved(down, "x", 3)
    near = moved(late[:, :cut] + from_below[:, :cut], "x", 1)
    far = moved(late[:, cut:] + from_above[:, cut:], "x", 3)
    first = own[:, :cut] + from_above[:, :cut] + near
    second = own[:, cut:] + from_below[:, cut:] + far
    return first, second


def shards(tmax, threshold, land_mask, region_id, block_fill, cell_area):
    members, days_in, cells = tmax.shape
    blocks = block_fill.shape[0]
    lanes = cells // blocks
    days = days_in - WINDOW + 1
    x = tmax.reshape(members, days_in, blocks, lanes).transpose(1, 2, 0, 3)
    x = x.reshape(days_in, blocks * members, lanes)
    threshold, land_mask, region_id, cell_area = (
        a.reshape(blocks, lanes) for a in (threshold, land_mask, region_id, cell_area)
    )
    *terms, sums = call(
        fold_kernel, block_fill, x, (threshold, land_mask, region_id, cell_area), PARTS, True
    )
    first, second = sum_over_members(*terms)
    mine, other = sum_over_cells(sums)
    cell_mean = jnp.concatenate([first, second], axis=1).reshape(-1, cells)
    region_index, land_count = pl.pallas_call(
        table_kernel,
        out_shape=[
            jax.ShapeDtypeStruct((REGIONS, members, days), jnp.float32),
            jax.ShapeDtypeStruct((1, REGIONS), jnp.int32),
        ],
        scratch_shapes=[pltpu.VMEM((SLOTS * 2 * members, 2 * HALF), jnp.float32)],
        compiler_params=pltpu.CompilerParams(vmem_limit_bytes=4 * 1024 * 1024),
    )(mine, other)
    return region_index.transpose(1, 2, 0), cell_mean, land_count.reshape(REGIONS)


def solution(mesh):
    devices = mesh.devices.reshape(4, 8, 2, 4)
    fine = Mesh(devices, ("y", "z", "core", "x"))
    cells = P(CELL_AXES)
    return jax.shard_map(
        shards,
        mesh=fine,
        in_specs=(P("x", None, CELL_AXES), cells, cells, cells, cells, cells),
        out_specs=(P("x", None, None), P("x", CELL_AXES), P()),
        check_vma=False,
    )
```

time: 51.7 us -> 42.6 us (0.82)
  waiting for transfers between devices: 14.9 us -> 6.75 us
  local copies, waits for them, and re-layouts: 5.53 us -> 1.67 us
  starting transfers between devices: 22.4 us -> 25.3 us
  Pallas kernels: 6.86 us -> 7.81 us
  other arithmetic: 0.74 us -> 0.21 us
    ppermute x12 -> x13, waiting for transfers between devices: 14.9 us -> 6.75 us  [moved(): lax.ppermute(array, axis, [(i, (i + shift) % size) for i in range(size)])]
    unnamed x13 -> x4, local copies, waits for them, and re-layouts: 5.29 us -> 1.66 us
    ppermute x12 -> x13, starting transfers between devices: 22.4 us -> 25.3 us  [moved(): lax.ppermute(array, axis, [(i, (i + shift) % size) for i in range(size)])]
    pallas_call x1 -> x2, Pallas kernels: 6.86 us -> 7.81 us  [the longest x1 6.89 us: call(): pl.pallas_call(kernel, grid=(tiles // TILES,), in_specs=[pl.BlockSpec(mem...]
  transfers between devices with their start and end apart: 12 -> 13, of which waited for: 7 -> 6; matrix products, arithmetic and copies ran while one was open for 2% -> 0% of each run, Pallas kernels for 0% -> 2%
where the time goes in v2:
time: 42.6 us; the launch traced here: 42.4 us
  starting transfers between devices  25.3 us (59%)
  Pallas kernels  7.81 us (18%)
  waiting for transfers between devices  6.75 us (16%)
  local copies, waits for them, and re-layouts  1.67 us (4%)
  between operations  0.71 us (2%)
    ppermute x13, starting transfers between devices, moved(): lax.ppermute(array, axis, [(i, (i + shift) % size) for i in range(size)])  25.3 us
    pallas_call x1, Pallas kernels, call(): pl.pallas_call(kernel, grid=(tiles // TILES,), in_specs=[pl.BlockSpec(mem...  6.89 us
    ppermute x13, waiting for transfers between devices, moved(): lax.ppermute(array, axis, [(i, (i + shift) % size) for i in range(size)])  6.75 us
    unnamed x4, local copies, waits for them, and re-layouts  1.66 us
    pallas_call x1, Pallas kernels, shards(): pl.pallas_call(table_kernel, out_shape=[jax.ShapeDtypeStruct((REGIONS, me...  0.92 us
  transfers between devices with their start and end apart: 13, of which 6 were waited for; matrix products, arithmetic and copies ran while one was open for 0% of the time, Pallas kernels for 2%

profile of v2, /device:TPU:1, one launch (start us, length us, event | category | flops | bytes accessed | tf_op | source)
XLA Modules:
  0.0 42.4 jit_solution(860554287538929531)
XLA Ops:
  0.6 0.0 copy-start
  0.6 0.6 %copy-done = s32[32]{0:T(128)S(1)} copy-done((s32[32]{0:T(128)S(1)}, s32[32]{0:T(128)}, u32[]{:S(2)}) %copy-start) | copy-done | bytes 152
  1.3 6.9 %shard_map.85 = (f32[23,32,128]{2,1,0:T(8,128)S(1)}, f32[23,32,128]{2,1,0:T(8,128)S(1)}, f32[23,32,128]{2,1,0:T(8,128)S(1)}, f32[23,32,128]{2,1,0:T(8,128)S(1)}, f32[24,8,128]{2,1,0:T(8,128)S(1)}) custom-call(s32[32]{0:T(128)S(1)} %copy-done, f32[97,128,128]{2,1,0:T(8,128)} %bitcast.21, s32[32,128]{1,0:T(8,128)} %bitcast.24, s32[32,128]{1,0:T(8,128)} %bitcast.25, ...), custom_call_target="tpu_custom_call" | custom-call | tf_op jit(solution)/shard_map/pallas_call | solution.py:151
  8.2 3.3 %collective-permute-start = (f32[12,8,128]{2,1,0:T(8,128)S(1)}, f32[12,8,128]{2,1,0:T(8,128)S(1)}, u32[]{:S(2)}, u32[]{:S(2)}) collective-permute-start(f32[12,8,128]{2,1,0:T(8,128)S(1)} %dynamic-slice_bitcast_fusion), channel_id=1, source_target_pairs={{0,4},{4,0},{1,5},{5,1},{2,6},{6,2},{3,7},{7,3},{8,12},{12,8},{9,1... | collective-permute-start | bytes 147464 | tf_op jit(solution)/shard_map/ppermute | solution.py:168
  11.5 0.9 %collective-permute-done = f32[12,8,128]{2,1,0:T(8,128)S(1)} collective-permute-done((f32[12,8,128]{2,1,0:T(8,128)S(1)}, f32[12,8,128]{2,1,0:T(8,128)S(1)}, u32[]{:S(2)}, u32[]{:S(2)}) %collective-permute-start) | collective-permute-done | bytes 49184 | tf_op jit(solution)/shard_map/ppermute | solution.py:168
  12.4 1.0 %collective-permute-start.3 = (f32[12,8,128]{2,1,0:T(8,128)S(1)}, f32[12,8,128]{2,1,0:T(8,128)S(1)}, u32[]{:S(2)}, u32[]{:S(2)}) collective-permute-start(f32[12,8,128]{2,1,0:T(8,128)S(1)} %bitcast_add_fusion), channel_id=1, source_target_pairs={{0,192},{64,0},{128,64},{192,128},{1,193},{65,1},{129,65},{193,129... | collective-permute-start | bytes 147464 | tf_op jit(solution)/shard_map/ppermute | solution.py:168
  13.5 0.4 collective-permute-start.2
  13.8 0.7 %collective-permute-start.1 = (f32[12,8,128]{2,1,0:T(8,128)S(1)}, f32[12,8,128]{2,1,0:T(8,128)S(1)}, u32[]{:S(2)}, u32[]{:S(2)}) collective-permute-start(f32[12,8,128]{2,1,0:T(8,128)S(1)} %bitcast_add_fusion), channel_id=1, source_target_pairs={{0,64},{64,128},{128,192},{192,0},{1,65},{65,129},{129,193},{193,1... | collective-permute-start | bytes 147464 | tf_op jit(solution)/shard_map/ppermute | solution.py:168
  14.5 2.5 %collective-permute-start.9 = (f32[23,32,128]{2,1,0:T(8,128)S(1)}, f32[23,32,128]{2,1,0:T(8,128)S(1)}, u32[]{:S(2)}, u32[]{:S(2)}) collective-permute-start(f32[23,32,128]{2,1,0:T(8,128)S(1)} %get-tuple-element.13), channel_id=1, source_target_pairs={{0,3},{1,0},{2,1},{3,2},{4,7},{5,4},{6,5},{7,6},{8,11},{9,8},{10,9... | collective-permute-start | bytes 1130504 | tf_op jit(solution)/shard_map/ppermute | solution.py:168
  17.0 0.0 collective-permute-start.10
  17.0 0.0 collective-permute-done.3
  17.0 1.0 %collective-permute-done.2 = f32[12,8,128]{2,1,0:T(8,128)S(1)} collective-permute-done((f32[12,8,128]{2,1,0:T(8,128)S(1)}, f32[12,8,128]{2,1,0:T(8,128)S(1)}, u32[]{:S(2)}, u32[]{:S(2)}) %collective-permute-start.2) | collective-permute-done | bytes 49184 | tf_op jit(solution)/shard_map/ppermute | solution.py:168
  18.0 0.5 %collective-permute-done.1 = f32[12,8,128]{2,1,0:T(8,128)S(1)} collective-permute-done((f32[12,8,128]{2,1,0:T(8,128)S(1)}, f32[12,8,128]{2,1,0:T(8,128)S(1)}, u32[]{:S(2)}, u32[]{:S(2)}) %collective-permute-start.1) | collective-permute-done | bytes 49184 | tf_op jit(solution)/shard_map/ppermute | solution.py:168
  18.5 1.7 %collective-permute-start.5 = (f32[12,8,128]{2,1,0:T(8,128)S(1)}, f32[12,8,128]{2,1,0:T(8,128)S(1)}, u32[]{:S(2)}, u32[]{:S(2)}) collective-permute-start(f32[12,8,128]{2,1,0:T(8,128)S(1)} %add_add_fusion.1), channel_id=1, source_target_pairs={{0,8},{8,16},{16,24},{24,32},{32,40},{40,48},{48,56},{56,0},{1,9},... | collective-permute-start | bytes 147464 | tf_op jit(solution)/shard_map/ppermute | solution.py:168
  20.2 4.0 %collective-permute-start.4 = (f32[12,8,128]{2,1,0:T(8,128)S(1)}, f32[12,8,128]{2,1,0:T(8,128)S(1)}, u32[]{:S(2)}, u32[]{:S(2)}) collective-permute-start(f32[12,8,128]{2,1,0:T(8,128)S(1)} %add_add_fusion.1), channel_id=1, source_target_pairs={{0,56},{8,0},{16,8},{24,16},{32,24},{40,32},{48,40},{56,48},{1,57}... | collective-permute-start | bytes 147464 | tf_op jit(solution)/shard_map/ppermute | solution.py:168
  24.2 1.7 %collective-permute-done.5 = f32[12,8,128]{2,1,0:T(8,128)S(1)} collective-permute-done((f32[12,8,128]{2,1,0:T(8,128)S(1)}, f32[12,8,128]{2,1,0:T(8,128)S(1)}, u32[]{:S(2)}, u32[]{:S(2)}) %collective-permute-start.5) | collective-permute-done | bytes 49184 | tf_op jit(solution)/shard_map/ppermute | solution.py:168
  25.9 0.0 collective-permute-done.4
  25.9 4.4 %collective-permute-start.7 = (f32[12,8,128]{2,1,0:T(8,128)S(1)}, f32[12,8,128]{2,1,0:T(8,128)S(1)}, u32[]{:S(2)}, u32[]{:S(2)}) collective-permute-start(f32[12,8,128]{2,1,0:T(8,128)S(1)} %get-tuple-element.18), channel_id=1, source_target_pairs={{0,24},{8,32},{16,40},{24,48},{32,56},{40,0},{48,8},{56,16},{1,25}... | collective-permute-start | bytes 147464 | tf_op jit(solution)/shard_map/ppermute | solution.py:168
  30.3 0.2 collective-permute-start.6
  30.5 0.0 collective-permute-done.9
  30.5 0.0 collective-permute-done.10
  30.5 0.1 slice_add_fusion.2
  30.5 1.0 %collective-permute-start.11 = (f32[23,16,128]{2,1,0:T(8,128)S(1)}, f32[23,16,128]{2,1,0:T(8,128)S(1)}, u32[]{:S(2)}, u32[]{:S(2)}) collective-permute-start(f32[23,16,128]{2,1,0:T(8,128)S(1)} %get-tuple-element.21), channel_id=1, source_target_pairs={{0,1},{1,2},{2,3},{3,0},{4,5},{5,6},{6,7},{7,4},{8,9},{9,10},{10,1... | collective-permute-start | bytes 565256 | tf_op jit(solution)/shard_map/ppermute | solution.py:168
  31.5 1.8 %collective-permute-start.12 = (f32[23,16,128]{2,1,0:T(8,128)S(1)}, f32[23,16,128]{2,1,0:T(8,128)S(1)}, u32[]{:S(2)}, u32[]{:S(2)}) collective-permute-start(f32[23,16,128]{2,1,0:T(8,128)S(1)} %get-tuple-element.22), channel_id=1, source_target_pairs={{0,3},{1,0},{2,1},{3,2},{4,7},{5,4},{6,5},{7,6},{8,11},{9,8},{10,9... | collective-permute-start | bytes 565256 | tf_op jit(solution)/shard_map/ppermute | solution.py:168
  33.3 0.0 collective-permute-done.7
  33.3 1.8 %collective-permute-done.6 = f32[12,8,128]{2,1,0:T(8,128)S(1)} collective-permute-done((f32[12,8,128]{2,1,0:T(8,128)S(1)}, f32[12,8,128]{2,1,0:T(8,128)S(1)}, u32[]{:S(2)}, u32[]{:S(2)}) %collective-permute-start.6) | collective-permute-done | bytes 49184 | tf_op jit(solution)/shard_map/ppermute | solution.py:168
  35.1 4.4 %collective-permute-start.8 = (f32[12,8,128]{2,1,0:T(8,128)S(1)}, f32[12,8,128]{2,1,0:T(8,128)S(1)}, u32[]{:S(2)}, u32[]{:S(2)}) collective-permute-start(f32[12,8,128]{2,1,0:T(8,128)S(1)} %add_add_fusion.mine_ref), channel_id=1, source_target_pairs={{0,4},{4,0},{1,5},{5,1},{2,6},{6,2},{3,7},{7,3},{8,12},{12,8},{9,1... | collective-permute-start | bytes 147464 | tf_op jit(solution)/shard_map/ppermute | solution.py:168
  39.5 0.9 %collective-permute-done.8.other_ref = f32[12,8,128]{2,1,0:T(8,128)S(1)} collective-permute-done((f32[12,8,128]{2,1,0:T(8,128)S(1)}, f32[12,8,128]{2,1,0:T(8,128)S(1)}, u32[]{:S(2)}, u32[]{:S(2)}) %collective-permute-start.8) | collective-permute-done | bytes 49184 | tf_op jit(solution)/shard_map/ppermute | solution.py:168
  40.4 0.9 %shard_map.86 = (f32[46,4,92]{2,1,0:T(4,128)}, s32[1,46]{1,0:T(1,128)}) custom-call(f32[12,8,128]{2,1,0:T(8,128)S(1)} %add_add_fusion.mine_ref, f32[12,8,128]{2,1,0:T(8,128)S(1)} %collective-permute-done.8.other_ref), custom_call_target="tpu_custom_call" | custom-call | tf_op jit(solution)/shard_map/pallas_call | solution.py:211
  41.3 0.0 collective-permute-done.11
  41.3 0.0 collective-permute-done.12
  41.3 0.1 fusion.1
  41.5 1.0 %copy.10 = f32[3,8,32,128]{3,1,2,0:T(8,128)} copy(f32[3,8,32,128]{3,2,1,0:T(8,128)S(1)} %bitcast.22) | data formatting | bytes 786432
  (7 shorter events, 0.1 us)
Async XLA Ops:
  0.6 0.7 %copy-start = (s32[32]{0:T(128)S(1)}, s32[32]{0:T(128)}, u32[]{:S(2)}) copy-start(s32[32]{0:T(128)} %fill_ref.1) | copy-start | bytes 388
  8.2 4.2 %collective-permute-start = (f32[12,8,128]{2,1,0:T(8,128)S(1)}, f32[12,8,128]{2,1,0:T(8,128)S(1)}, u32[]{:S(2)}, u32[]{:S(2)}) collective-permute-start(f32[12,8,128]{2,1,0:T(8,128)S(1)} %dynamic-slice_bitcast_fusion), channel_id=1, source_target_pairs={{0,4},{4,0},{1,5},{5,1},{2,6},{6,2},{3,7},{7,3},{8,12},{12,8},{9,1... | collective-permute-start | bytes 147464 | tf_op jit(solution)/shard_map/ppermute | solution.py:168
  12.4 4.6 %collective-permute-start.3 = (f32[12,8,128]{2,1,0:T(8,128)S(1)}, f32[12,8,128]{2,1,0:T(8,128)S(1)}, u32[]{:S(2)}, u32[]{:S(2)}) collective-permute-start(f32[12,8,128]{2,1,0:T(8,128)S(1)} %bitcast_add_fusion), channel_id=1, source_target_pairs={{0,192},{64,0},{128,64},{192,128},{1,193},{65,1},{129,65},{193,129... | collective-permute-start | bytes 147464 | tf_op jit(solution)/shard_map/ppermute | solution.py:168
  13.5 4.5 %collective-permute-start.2 = (f32[12,8,128]{2,1,0:T(8,128)S(1)}, f32[12,8,128]{2,1,0:T(8,128)S(1)}, u32[]{:S(2)}, u32[]{:S(2)}) collective-permute-start(f32[12,8,128]{2,1,0:T(8,128)S(1)} %bitcast_add_fusion), channel_id=1, source_target_pairs={{0,128},{64,192},{128,0},{192,64},{1,129},{65,193},{129,1},{193,65... | collective-permute-start | bytes 147464 | tf_op jit(solution)/shard_map/ppermute | solution.py:168
  13.8 4.6 %collective-permute-start.1 = (f32[12,8,128]{2,1,0:T(8,128)S(1)}, f32[12,8,128]{2,1,0:T(8,128)S(1)}, u32[]{:S(2)}, u32[]{:S(2)}) collective-permute-start(f32[12,8,128]{2,1,0:T(8,128)S(1)} %bitcast_add_fusion), channel_id=1, source_target_pairs={{0,64},{64,128},{128,192},{192,0},{1,65},{65,129},{129,193},{193,1... | collective-permute-start | bytes 147464 | tf_op jit(solution)/shard_map/ppermute | solution.py:168
  14.5 15.9 %collective-permute-start.9 = (f32[23,32,128]{2,1,0:T(8,128)S(1)}, f32[23,32,128]{2,1,0:T(8,128)S(1)}, u32[]{:S(2)}, u32[]{:S(2)}) collective-permute-start(f32[23,32,128]{2,1,0:T(8,128)S(1)} %get-tuple-element.13), channel_id=1, source_target_pairs={{0,3},{1,0},{2,1},{3,2},{4,7},{5,4},{6,5},{7,6},{8,11},{9,8},{10,9... | collective-permute-start | bytes 1130504 | tf_op jit(solution)/shard_map/ppermute | solution.py:168
  17.0 13.5 %collective-permute-start.10 = (f32[23,32,128]{2,1,0:T(8,128)S(1)}, f32[23,32,128]{2,1,0:T(8,128)S(1)}, u32[]{:S(2)}, u32[]{:S(2)}) collective-permute-start(f32[23,32,128]{2,1,0:T(8,128)S(1)} %get-tuple-element.15), channel_id=1, source_target_pairs={{0,1},{1,2},{2,3},{3,0},{4,5},{5,6},{6,7},{7,4},{8,9},{9,10},{10,1... | collective-permute-start | bytes 1130504 | tf_op jit(solution)/shard_map/ppermute | solution.py:168
  18.5 7.4 %collective-permute-start.5 = (f32[12,8,128]{2,1,0:T(8,128)S(1)}, f32[12,8,128]{2,1,0:T(8,128)S(1)}, u32[]{:S(2)}, u32[]{:S(2)}) collective-permute-start(f32[12,8,128]{2,1,0:T(8,128)S(1)} %add_add_fusion.1), channel_id=1, source_target_pairs={{0,8},{8,16},{16,24},{24,32},{32,40},{40,48},{48,56},{56,0},{1,9},... | collective-permute-start | bytes 147464 | tf_op jit(solution)/shard_map/ppermute | solution.py:168
  20.2 5.7 %collective-permute-start.4 = (f32[12,8,128]{2,1,0:T(8,128)S(1)}, f32[12,8,128]{2,1,0:T(8,128)S(1)}, u32[]{:S(2)}, u32[]{:S(2)}) collective-permute-start(f32[12,8,128]{2,1,0:T(8,128)S(1)} %add_add_fusion.1), channel_id=1, source_target_pairs={{0,56},{8,0},{16,8},{24,16},{32,24},{40,32},{48,40},{56,48},{1,57}... | collective-permute-start | bytes 147464 | tf_op jit(solution)/shard_map/ppermute | solution.py:168
  25.9 7.4 %collective-permute-start.7 = (f32[12,8,128]{2,1,0:T(8,128)S(1)}, f32[12,8,128]{2,1,0:T(8,128)S(1)}, u32[]{:S(2)}, u32[]{:S(2)}) collective-permute-start(f32[12,8,128]{2,1,0:T(8,128)S(1)} %get-tuple-element.18), channel_id=1, source_target_pairs={{0,24},{8,32},{16,40},{24,48},{32,56},{40,0},{48,8},{56,16},{1,25}... | collective-permute-start | bytes 147464 | tf_op jit(solution)/shard_map/ppermute | solution.py:168
  30.3 4.9 %collective-permute-start.6 = (f32[12,8,128]{2,1,0:T(8,128)S(1)}, f32[12,8,128]{2,1,0:T(8,128)S(1)}, u32[]{:S(2)}, u32[]{:S(2)}) collective-permute-start(f32[12,8,128]{2,1,0:T(8,128)S(1)} %get-tuple-element.17), channel_id=1, source_target_pairs={{0,40},{8,48},{16,56},{24,0},{32,8},{40,16},{48,24},{56,32},{1,41}... | collective-permute-start | bytes 147464 | tf_op jit(solution)/shard_map/ppermute | solution.py:168
  30.5 10.8 %collective-permute-start.11 = (f32[23,16,128]{2,1,0:T(8,128)S(1)}, f32[23,16,128]{2,1,0:T(8,128)S(1)}, u32[]{:S(2)}, u32[]{:S(2)}) collective-permute-start(f32[23,16,128]{2,1,0:T(8,128)S(1)} %get-tuple-element.21), channel_id=1, source_target_pairs={{0,1},{1,2},{2,3},{3,0},{4,5},{5,6},{6,7},{7,4},{8,9},{9,10},{10,1... | collective-permute-start | bytes 565256 | tf_op jit(solution)/shard_map/ppermute | solution.py:168
  31.5 9.8 %collective-permute-start.12 = (f32[23,16,128]{2,1,0:T(8,128)S(1)}, f32[23,16,128]{2,1,0:T(8,128)S(1)}, u32[]{:S(2)}, u32[]{:S(2)}) collective-permute-start(f32[23,16,128]{2,1,0:T(8,128)S(1)} %get-tuple-element.22), channel_id=1, source_target_pairs={{0,3},{1,0},{2,1},{3,2},{4,7},{5,4},{6,5},{7,6},{8,11},{9,8},{10,9... | collective-permute-start | bytes 565256 | tf_op jit(solution)/shard_map/ppermute | solution.py:168
  35.1 5.2 %collective-permute-start.8 = (f32[12,8,128]{2,1,0:T(8,128)S(1)}, f32[12,8,128]{2,1,0:T(8,128)S(1)}, u32[]{:S(2)}, u32[]{:S(2)}) collective-permute-start(f32[12,8,128]{2,1,0:T(8,128)S(1)} %add_add_fusion.mine_ref), channel_id=1, source_target_pairs={{0,4},{4,0},{1,5},{5,1},{2,6},{6,2},{3,7},{7,3},{8,12},{12,8},{9,1... | collective-permute-start | bytes 147464 | tf_op jit(solution)/shard_map/ppermute | solution.py:168

commit v3 on v2

--- a/solution.py
+++ b/solution.py
@@ -10,29 +10,63 @@
 HALF = 64
 PARTS = 4
 SLOTS = 24
-TILES = 8
+TILES = 16
+CHUNK = 8
 CELL_AXES = ("y", "z", "core")
 
 
 def live_cells(fill_ref, mask_ref, step):
     tiles, lanes = mask_ref.shape
-    sub = lax.broadcasted_iota(jnp.int32, (tiles, lanes), 0)
+    blocks = fill_ref.shape[1]
+    row = lax.broadcasted_iota(jnp.int32, (tiles, blocks), 0) + step * tiles
+    here = row == lax.broadcasted_iota(jnp.int32, (tiles, blocks), 1)
+    fill = jnp.where(here, fill_ref[...].astype(jnp.float32), 0.0)
+    fill = jnp.sum(fill, axis=1, keepdims=True).astype(jnp.int32)
     lane = lax.broadcasted_iota(jnp.int32, (tiles, lanes), 1)
-    fill = jnp.zeros((tiles, lanes), jnp.int32)
-    for r in range(tiles):
-        fill = jnp.where(sub == r, fill_ref[step * tiles + r], fill)
     return jnp.where(lane < fill, mask_ref[...], 0).astype(jnp.float32)
 
 
-def cell_sums(step, x_ref, live, limit, outs, total_ref):
+def excess_terms(x_ref, weight, live, limit, excess_ref, left_ref):
+    days_in = x_ref.shape[0]
     tiles, lanes = live.shape
     members = x_ref.shape[1] // tiles
+    group = 2 * members
+    width = tiles // 2 * lanes
+
+    def spread(v, t):
+        rows = [jnp.broadcast_to(v[r : r + 1], (members, lanes)) for r in (t, t + 1)]
+        return jnp.concatenate(rows, axis=0)
+
+    for p in range(tiles // 2):
+        w8, l8, t8 = spread(weight, 2 * p), spread(live, 2 * p), spread(limit, 2 * p)
+
+        def keep(first, v):
+            high = v.astype(jnp.bfloat16)
+            low = (v - high.astype(jnp.float32)).astype(jnp.bfloat16)
+            left_ref[first : first + v.shape[0], p * lanes : (p + 1) * lanes] = high
+            left_ref[first : first + v.shape[0], width + p * lanes : width + (p + 1) * lanes] = low
+
+        for d in range(0, days_in, CHUNK):
+            n = min(CHUNK, days_in - d)
+            e = jnp.maximum(x_ref[d : d + n, p * group : (p + 1) * group, :] - t8[None], 0.0)
+            excess_ref[d : d + n, p * group : (p + 1) * group, :] = e
+            rows = (e * w8[None]).reshape(n * group, lanes)
+            if d + n == days_in:
+                rows = jnp.concatenate([rows, w8, l8, jnp.zeros((left_ref.shape[0] - (days_in + 2) * group, lanes), jnp.float32)], axis=0)
+            keep(d * group, rows)
+
+
+def cell_sums(step, excess_ref, live, outs, total_ref):
+    days_in = excess_ref.shape[0]
+    tiles, lanes = live.shape
+    members = excess_ref.shape[1] // tiles
     block_days = outs[0].shape[0]
-    total = None
-    for m in range(members):
-        one = jnp.maximum(x_ref[:, pl.ds(m, tiles, stride=members), :] - limit[None], 0.0)
-        total = one if total is None else total + one
-    total_ref[...] = total
+    for d in range(0, days_in, CHUNK):
+        n = min(CHUNK, days_in - d)
+        total = excess_ref[d : d + n, pl.ds(0, tiles, stride=members), :]
+        for m in range(1, members):
+            total = total + excess_ref[d : d + n, pl.ds(m, tiles, stride=members), :]
+        total_ref[d : d + n] = total
     me = lax.axis_index("x")
     scale = live * (1.0 / (WINDOW * members * PARTS))
     early = (2 * step < pl.num_programs(0)).astype(jnp.int32)
@@ -45,38 +79,20 @@
         out[...] = rolled * scale[None]
 
 
-def region_sums(step, x_ref, live, weight, limit, rid_ref, sums_ref, acc_ref):
-    days_in = x_ref.shape[0]
-    tiles, lanes = live.shape
-    members = x_ref.shape[1] // tiles
-    group = 2 * members
+def region_sums(step, left_ref, rid_ref, acc_ref):
+    tiles, lanes = rid_ref.shape
     region = lax.broadcasted_iota(jnp.int32, (HALF, lanes), 0)
 
-    def spread(v, t):
-        rows = [jnp.broadcast_to(v[r : r + 1], (members, lanes)) for r in (t, t + 1)]
-        return jnp.concatenate(rows, axis=0)
-
-    part = None
-    for pair in range(0, tiles // 2, 2):
-        lefts, rights = [], []
-        for p in (pair, pair + 1):
-            w8, l8, t8 = spread(weight, 2 * p), spread(live, 2 * p), spread(limit, 2 * p)
-            x = x_ref[:, p * group : (p + 1) * group, :]
-            e = jnp.maximum(x - t8[None], 0.0) * w8[None]
-            e = e.reshape(days_in * group, lanes)
-            lefts.append(jnp.concatenate([e, w8, l8], axis=0))
-            hot = [
-                (region == rid_ref[t : t + 1, :]).astype(jnp.float32) for t in (2 * p, 2 * p + 1)
-            ]
-            rights.append(jnp.concatenate(hot, axis=0))
-        left = jnp.concatenate(lefts, axis=1)
-        right = jnp.concatenate(rights, axis=1).astype(jnp.bfloat16)
-        high = left.astype(jnp.bfloat16)
-        low = (left - high.astype(jnp.float32)).astype(jnp.bfloat16)
-        dims = (((1,), (1,)), ((), ()))
-        both = lax.dot_general(high, right, dims, preferred_element_type=jnp.float32)
-        both = both + lax.dot_general(low, right, dims, preferred_element_type=jnp.float32)
-        part = both if part is None else part + both
+    def hot(t):
+        return (region == rid_ref[t : t + 1, :]).astype(jnp.float32)
+
+    even = jnp.concatenate([hot(t) for t in range(0, tiles, 2)], axis=1)
+    odd = jnp.concatenate([hot(t) for t in range(1, tiles, 2)], axis=1)
+    right = jnp.concatenate([even, odd], axis=0).astype(jnp.bfloat16)
+    right = jnp.concatenate([right, right], axis=1)
+    part = lax.dot_general(
+        left_ref[...], right, (((1,), (1,)), ((), ())), preferred_element_type=jnp.float32
+    )
 
     @pl.when(step == 0)
     def _():
@@ -86,30 +102,37 @@
     def _():
         acc_ref[...] += part
 
-    @pl.when(step == pl.num_programs(0) - 1)
-    def _():
-        days = days_in - WINDOW + 1
-        v = acc_ref[...].reshape(days_in + 2, group, 2 * HALF)
-        pair = v[: days_in - 1] + v[1:days_in]
-        rolled = (pair[0:days] + pair[2 : 2 + days] + pair[4 : 4 + days]) * (1.0 / WINDOW)
-        pad = jnp.zeros((4 * SLOTS - days - 2, group, 2 * HALF), jnp.float32)
-        v = jnp.concatenate([rolled, v[days_in:], pad], axis=0)
-        s = v + pltpu.roll(pltpu.roll(v, members, 1), HALF, 2)
-        r = pltpu.roll(s, HALF, 2)
-        top = lax.broadcasted_iota(jnp.int32, (SLOTS, group, 2 * HALF), 1) < members
-        low = lax.broadcasted_iota(jnp.int32, (SLOTS, group, 2 * HALF), 2) < HALF
-        upper = jnp.where(low, s[0:SLOTS], r[SLOTS : 2 * SLOTS])
-        lower = jnp.where(low, r[2 * SLOTS : 3 * SLOTS], s[3 * SLOTS :])
-        sums_ref[...] = jnp.where(top, upper, lower)
+
+def packed_sums(acc_ref, sums_ref, days_in):
+    group = sums_ref.shape[1]
+    members = group // 2
+    days = days_in - WINDOW + 1
+    v = acc_ref[: (days_in + 2) * group].reshape(days_in + 2, group, 2 * HALF)
+    pair = v[: days_in - 1] + v[1:days_in]
+    rolled = (pair[0:days] + pair[2 : 2 + days] + pair[4 : 4 + days]) * (1.0 / WINDOW)
+    pad = jnp.zeros((4 * SLOTS - days - 2, group, 2 * HALF), jnp.float32)
+    v = jnp.concatenate([rolled, v[days_in:], pad], axis=0)
+    s = v + pltpu.roll(pltpu.roll(v, members, 1), HALF, 2)
+    r = pltpu.roll(s, HALF, 2)
+    top = lax.broadcasted_iota(jnp.int32, (SLOTS, group, 2 * HALF), 1) < members
+    low = lax.broadcasted_iota(jnp.int32, (SLOTS, group, 2 * HALF), 2) < HALF
+    upper = jnp.where(low, s[0:SLOTS], r[SLOTS : 2 * SLOTS])
+    lower = jnp.where(low, r[2 * SLOTS : 3 * SLOTS], s[3 * SLOTS :])
+    sums_ref[...] = jnp.where(top, upper, lower)
 
 
 def fold_kernel(fill_ref, x_ref, thr_ref, mask_ref, rid_ref, area_ref, *refs):
-    *outs, sums_ref, acc_ref, total_ref = refs
+    *outs, sums_ref, acc_ref, total_ref, excess_ref, left_ref = refs
     step = pl.program_id(0)
     live = live_cells(fill_ref, mask_ref, step)
     limit = thr_ref[...].astype(jnp.float32) * 0.1
-    cell_sums(step, x_ref, live, limit, outs, total_ref)
-    region_sums(step, x_ref, live, area_ref[...] * live, limit, rid_ref, sums_ref, acc_ref)
+    excess_terms(x_ref, area_ref[...] * live, live, limit, excess_ref, left_ref)
+    region_sums(step, left_ref, rid_ref, acc_ref)
+    cell_sums(step, excess_ref, live, outs, total_ref)
+
+    @pl.when(step == pl.num_programs(0) - 1)
+    def _():
+        packed_sums(acc_ref, sums_ref, x_ref.shape[0])
 
 
 def table_kernel(mine_ref, other_ref, index_ref, count_ref, rows_ref):
@@ -145,14 +168,18 @@
         sums = (SLOTS, 2 * members, 2 * HALF)
         out_specs.append(pl.BlockSpec(sums, lambda i: (0, 0, 0)))
         out_shape.append(jax.ShapeDtypeStruct(sums, jnp.float32))
-        scratch.append(pltpu.VMEM(((days_in + 2) * 2 * members, 2 * HALF), jnp.float32))
-    if blocks:
-        scratch.append(pltpu.VMEM((days_in, TILES, lanes), jnp.float32))
+        high = -(-(days_in + 2) * 2 * members // 16) * 16
+        scratch = [
+            pltpu.VMEM((high, 2 * HALF), jnp.float32),
+            pltpu.VMEM((days_in, TILES, lanes), jnp.float32),
+            pltpu.VMEM((days_in, TILES * members, lanes), jnp.float32),
+            pltpu.VMEM((high, TILES * lanes), jnp.bfloat16),
+        ]
     return pl.pallas_call(
         kernel,
         grid=(tiles // TILES,),
         in_specs=[
-            pl.BlockSpec(memory_space=pltpu.SMEM),
+            pl.BlockSpec(fill.shape, lambda i: (0, 0)),
             pl.BlockSpec((days_in, TILES * members, lanes), lambda i: (0, i, 0)),
         ]
         + [flat] * len(flats),
@@ -160,7 +187,7 @@
         out_shape=out_shape,
         scratch_shapes=scratch,
         compiler_params=pltpu.CompilerParams(vmem_limit_bytes=40 * 1024 * 1024),
-    )(*[pltpu.with_memory_space_constraint(a, pltpu.HBM) if a is not fill else a for a in (fill, x, *flats)])
+    )(*[pltpu.with_memory_space_constraint(a, pltpu.HBM) for a in (fill, x, *flats)])
 
 
 def moved(array, axis, shift):
@@ -203,7 +230,7 @@
         a.reshape(blocks, lanes) for a in (threshold, land_mask, region_id, cell_area)
     )
     *terms, sums = call(
-        fold_kernel, block_fill, x, (threshold, land_mask, region_id, cell_area), PARTS, True
+        fold_kernel, block_fill.reshape(1, blocks), x, (threshold, land_mask, region_id, cell_area), PARTS, True
     )
     first, second = sum_over_members(*terms)
     mine, other = sum_over_cells(sums)

time: 42.6 us -> 41.1 us (0.965)
  Pallas kernels: 7.81 us -> 7.02 us
  local copies, waits for them, and re-layouts: 1.67 us -> 1.02 us
    pallas_call x1, Pallas kernels: 6.89 us -> 6.1 us  [call(): pl.pallas_call(kernel, grid=(tiles // TILES,), in_specs=[pl.BlockSpec(fil...]
    unnamed x4 -> x2, local copies, waits for them, and re-layouts: 1.66 us -> 1.01 us
where the time goes in v3:
time: 41.1 us; the launch traced here: 41 us
  starting transfers between devices  25.3 us (62%)
  Pallas kernels  7.02 us (17%)
  waiting for transfers between devices  6.75 us (16%)
  local copies, waits for them, and re-layouts  1.02 us (2%)
  between operations  0.7 us (2%)
    ppermute x13, starting transfers between devices, moved(): lax.ppermute(array, axis, [(i, (i + shift) % size) for i in range(size)])  25.3 us
    ppermute x13, waiting for transfers between devices, moved(): lax.ppermute(array, axis, [(i, (i + shift) % size) for i in range(size)])  6.75 us
    pallas_call x1, Pallas kernels, call(): pl.pallas_call(kernel, grid=(tiles // TILES,), in_specs=[pl.BlockSpec(fil...  6.1 us
    unnamed x2, local copies, waits for them, and re-layouts  1.01 us
    pallas_call x1, Pallas kernels, shards(): pl.pallas_call(table_kernel, out_shape=[jax.ShapeDtypeStruct((REGIONS, me...  0.92 us
  transfers between devices with their start and end apart: 13, of which 6 were waited for; matrix products, arithmetic and copies ran while one was open for 0% of the time, Pallas kernels for 2%

profile of v3, /device:TPU:1, one launch (start us, length us, event | category | flops | bytes accessed | tf_op | source)
XLA Modules:
  0.0 41.0 jit_solution(3366512287507557536)
XLA Ops:
  0.6 6.1 %shard_map.85 = (f32[23,32,128]{2,1,0:T(8,128)S(1)}, f32[23,32,128]{2,1,0:T(8,128)S(1)}, f32[23,32,128]{2,1,0:T(8,128)S(1)}, f32[23,32,128]{2,1,0:T(8,128)S(1)}, f32[24,8,128]{2,1,0:T(8,128)S(1)}) custom-call(s32[1,32]{1,0:T(1,128)} %bitcast.29, f32[97,128,128]{2,1,0:T(8,128)} %bitcast.22, s32[32,128]{1,0:T(8,128)} %bitcast.25, s32[32,128]{1,0:T(8,128)} %bitcast.26, ...), custom_call_target="tpu_custom_call" | custom-call | tf_op jit(solution)/shard_map/pallas_call | solution.py:178
  6.8 3.3 %collective-permute-start = (f32[12,8,128]{2,1,0:T(8,128)S(1)}, f32[12,8,128]{2,1,0:T(8,128)S(1)}, u32[]{:S(2)}, u32[]{:S(2)}) collective-permute-start(f32[12,8,128]{2,1,0:T(8,128)S(1)} %dynamic-slice_bitcast_fusion), channel_id=1, source_target_pairs={{0,4},{4,0},{1,5},{5,1},{2,6},{6,2},{3,7},{7,3},{8,12},{12,8},{9,1... | collective-permute-start | bytes 147464 | tf_op jit(solution)/shard_map/ppermute | solution.py:195
  10.1 0.9 %collective-permute-done = f32[12,8,128]{2,1,0:T(8,128)S(1)} collective-permute-done((f32[12,8,128]{2,1,0:T(8,128)S(1)}, f32[12,8,128]{2,1,0:T(8,128)S(1)}, u32[]{:S(2)}, u32[]{:S(2)}) %collective-permute-start) | collective-permute-done | bytes 49184 | tf_op jit(solution)/shard_map/ppermute | solution.py:195
  11.0 1.0 %collective-permute-start.3 = (f32[12,8,128]{2,1,0:T(8,128)S(1)}, f32[12,8,128]{2,1,0:T(8,128)S(1)}, u32[]{:S(2)}, u32[]{:S(2)}) collective-permute-start(f32[12,8,128]{2,1,0:T(8,128)S(1)} %bitcast_add_fusion), channel_id=1, source_target_pairs={{0,192},{64,0},{128,64},{192,128},{1,193},{65,1},{129,65},{193,129... | collective-permute-start | bytes 147464 | tf_op jit(solution)/shard_map/ppermute | solution.py:195
  12.0 0.4 collective-permute-start.2
  12.4 0.7 %collective-permute-start.1 = (f32[12,8,128]{2,1,0:T(8,128)S(1)}, f32[12,8,128]{2,1,0:T(8,128)S(1)}, u32[]{:S(2)}, u32[]{:S(2)}) collective-permute-start(f32[12,8,128]{2,1,0:T(8,128)S(1)} %bitcast_add_fusion), channel_id=1, source_target_pairs={{0,64},{64,128},{128,192},{192,0},{1,65},{65,129},{129,193},{193,1... | collective-permute-start | bytes 147464 | tf_op jit(solution)/shard_map/ppermute | solution.py:195
  13.1 2.5 %collective-permute-start.9 = (f32[23,32,128]{2,1,0:T(8,128)S(1)}, f32[23,32,128]{2,1,0:T(8,128)S(1)}, u32[]{:S(2)}, u32[]{:S(2)}) collective-permute-start(f32[23,32,128]{2,1,0:T(8,128)S(1)} %get-tuple-element.13), channel_id=1, source_target_pairs={{0,3},{1,0},{2,1},{3,2},{4,7},{5,4},{6,5},{7,6},{8,11},{9,8},{10,9... | collective-permute-start | bytes 1130504 | tf_op jit(solution)/shard_map/ppermute | solution.py:195
  15.5 0.0 collective-permute-start.10
  15.5 0.0 collective-permute-done.3
  15.5 1.0 %collective-permute-done.2 = f32[12,8,128]{2,1,0:T(8,128)S(1)} collective-permute-done((f32[12,8,128]{2,1,0:T(8,128)S(1)}, f32[12,8,128]{2,1,0:T(8,128)S(1)}, u32[]{:S(2)}, u32[]{:S(2)}) %collective-permute-start.2) | collective-permute-done | bytes 49184 | tf_op jit(solution)/shard_map/ppermute | solution.py:195
  16.5 0.5 %collective-permute-done.1 = f32[12,8,128]{2,1,0:T(8,128)S(1)} collective-permute-done((f32[12,8,128]{2,1,0:T(8,128)S(1)}, f32[12,8,128]{2,1,0:T(8,128)S(1)}, u32[]{:S(2)}, u32[]{:S(2)}) %collective-permute-start.1) | collective-permute-done | bytes 49184 | tf_op jit(solution)/shard_map/ppermute | solution.py:195
  17.0 1.7 %collective-permute-start.5 = (f32[12,8,128]{2,1,0:T(8,128)S(1)}, f32[12,8,128]{2,1,0:T(8,128)S(1)}, u32[]{:S(2)}, u32[]{:S(2)}) collective-permute-start(f32[12,8,128]{2,1,0:T(8,128)S(1)} %add_add_fusion.1), channel_id=1, source_target_pairs={{0,8},{8,16},{16,24},{24,32},{32,40},{40,48},{48,56},{56,0},{1,9},... | collective-permute-start | bytes 147464 | tf_op jit(solution)/shard_map/ppermute | solution.py:195
  18.7 4.0 %collective-permute-start.4 = (f32[12,8,128]{2,1,0:T(8,128)S(1)}, f32[12,8,128]{2,1,0:T(8,128)S(1)}, u32[]{:S(2)}, u32[]{:S(2)}) collective-permute-start(f32[12,8,128]{2,1,0:T(8,128)S(1)} %add_add_fusion.1), channel_id=1, source_target_pairs={{0,56},{8,0},{16,8},{24,16},{32,24},{40,32},{48,40},{56,48},{1,57}... | collective-permute-start | bytes 147464 | tf_op jit(solution)/shard_map/ppermute | solution.py:195
  22.7 1.7 %collective-permute-done.5 = f32[12,8,128]{2,1,0:T(8,128)S(1)} collective-permute-done((f32[12,8,128]{2,1,0:T(8,128)S(1)}, f32[12,8,128]{2,1,0:T(8,128)S(1)}, u32[]{:S(2)}, u32[]{:S(2)}) %collective-permute-start.5) | collective-permute-done | bytes 49184 | tf_op jit(solution)/shard_map/ppermute | solution.py:195
  24.4 0.0 collective-permute-done.4
  24.4 4.4 %collective-permute-start.7 = (f32[12,8,128]{2,1,0:T(8,128)S(1)}, f32[12,8,128]{2,1,0:T(8,128)S(1)}, u32[]{:S(2)}, u32[]{:S(2)}) collective-permute-start(f32[12,8,128]{2,1,0:T(8,128)S(1)} %get-tuple-element.18), channel_id=1, source_target_pairs={{0,24},{8,32},{16,40},{24,48},{32,56},{40,0},{48,8},{56,16},{1,25}... | collective-permute-start | bytes 147464 | tf_op jit(solution)/shard_map/ppermute | solution.py:195
  28.8 0.2 collective-permute-start.6
  29.0 0.0 collective-permute-done.9
  29.0 0.0 collective-permute-done.10
  29.0 0.1 slice_add_fusion.2
  29.1 1.0 %collective-permute-start.11 = (f32[23,16,128]{2,1,0:T(8,128)S(1)}, f32[23,16,128]{2,1,0:T(8,128)S(1)}, u32[]{:S(2)}, u32[]{:S(2)}) collective-permute-start(f32[23,16,128]{2,1,0:T(8,128)S(1)} %get-tuple-element.21), channel_id=1, source_target_pairs={{0,1},{1,2},{2,3},{3,0},{4,5},{5,6},{6,7},{7,4},{8,9},{9,10},{10,1... | collective-permute-start | bytes 565256 | tf_op jit(solution)/shard_map/ppermute | solution.py:195
  30.1 1.8 %collective-permute-start.12 = (f32[23,16,128]{2,1,0:T(8,128)S(1)}, f32[23,16,128]{2,1,0:T(8,128)S(1)}, u32[]{:S(2)}, u32[]{:S(2)}) collective-permute-start(f32[23,16,128]{2,1,0:T(8,128)S(1)} %get-tuple-element.22), channel_id=1, source_target_pairs={{0,3},{1,0},{2,1},{3,2},{4,7},{5,4},{6,5},{7,6},{8,11},{9,8},{10,9... | collective-permute-start | bytes 565256 | tf_op jit(solution)/shard_map/ppermute | solution.py:195
  31.8 0.0 collective-permute-done.7
  31.8 1.8 %collective-permute-done.6 = f32[12,8,128]{2,1,0:T(8,128)S(1)} collective-permute-done((f32[12,8,128]{2,1,0:T(8,128)S(1)}, f32[12,8,128]{2,1,0:T(8,128)S(1)}, u32[]{:S(2)}, u32[]{:S(2)}) %collective-permute-start.6) | collective-permute-done | bytes 49184 | tf_op jit(solution)/shard_map/ppermute | solution.py:195
  33.7 4.4 %collective-permute-start.8 = (f32[12,8,128]{2,1,0:T(8,128)S(1)}, f32[12,8,128]{2,1,0:T(8,128)S(1)}, u32[]{:S(2)}, u32[]{:S(2)}) collective-permute-start(f32[12,8,128]{2,1,0:T(8,128)S(1)} %add_add_fusion.mine_ref), channel_id=1, source_target_pairs={{0,4},{4,0},{1,5},{5,1},{2,6},{6,2},{3,7},{7,3},{8,12},{12,8},{9,1... | collective-permute-start | bytes 147464 | tf_op jit(solution)/shard_map/ppermute | solution.py:195
  38.0 0.9 %collective-permute-done.8.other_ref = f32[12,8,128]{2,1,0:T(8,128)S(1)} collective-permute-done((f32[12,8,128]{2,1,0:T(8,128)S(1)}, f32[12,8,128]{2,1,0:T(8,128)S(1)}, u32[]{:S(2)}, u32[]{:S(2)}) %collective-permute-start.8) | collective-permute-done | bytes 49184 | tf_op jit(solution)/shard_map/ppermute | solution.py:195
  38.9 0.9 %shard_map.86 = (f32[46,4,92]{2,1,0:T(4,128)}, s32[1,46]{1,0:T(1,128)}) custom-call(f32[12,8,128]{2,1,0:T(8,128)S(1)} %add_add_fusion.mine_ref, f32[12,8,128]{2,1,0:T(8,128)S(1)} %collective-permute-done.8.other_ref), custom_call_target="tpu_custom_call" | custom-call | tf_op jit(solution)/shard_map/pallas_call | solution.py:238
  39.8 0.0 collective-permute-done.11
  39.8 0.0 collective-permute-done.12
  39.8 0.1 fusion.1
  40.0 1.0 %copy.10 = f32[3,8,32,128]{3,1,2,0:T(8,128)} copy(f32[3,8,32,128]{3,2,1,0:T(8,128)S(1)} %bitcast.23) | data formatting | bytes 786432
  (7 shorter events, 0.1 us)
Async XLA Ops:
  6.8 4.2 %collective-permute-start = (f32[12,8,128]{2,1,0:T(8,128)S(1)}, f32[12,8,128]{2,1,0:T(8,128)S(1)}, u32[]{:S(2)}, u32[]{:S(2)}) collective-permute-start(f32[12,8,128]{2,1,0:T(8,128)S(1)} %dynamic-slice_bitcast_fusion), channel_id=1, source_target_pairs={{0,4},{4,0},{1,5},{5,1},{2,6},{6,2},{3,7},{7,3},{8,12},{12,8},{9,1... | collective-permute-start | bytes 147464 | tf_op jit(solution)/shard_map/ppermute | solution.py:195
  11.0 4.6 %collective-permute-start.3 = (f32[12,8,128]{2,1,0:T(8,128)S(1)}, f32[12,8,128]{2,1,0:T(8,128)S(1)}, u32[]{:S(2)}, u32[]{:S(2)}) collective-permute-start(f32[12,8,128]{2,1,0:T(8,128)S(1)} %bitcast_add_fusion), channel_id=1, source_target_pairs={{0,192},{64,0},{128,64},{192,128},{1,193},{65,1},{129,65},{193,129... | collective-permute-start | bytes 147464 | tf_op jit(solution)/shard_map/ppermute | solution.py:195
  12.0 4.5 %collective-permute-start.2 = (f32[12,8,128]{2,1,0:T(8,128)S(1)}, f32[12,8,128]{2,1,0:T(8,128)S(1)}, u32[]{:S(2)}, u32[]{:S(2)}) collective-permute-start(f32[12,8,128]{2,1,0:T(8,128)S(1)} %bitcast_add_fusion), channel_id=1, source_target_pairs={{0,128},{64,192},{128,0},{192,64},{1,129},{65,193},{129,1},{193,65... | collective-permute-start | bytes 147464 | tf_op jit(solution)/shard_map/ppermute | solution.py:195
  12.4 4.6 %collective-permute-start.1 = (f32[12,8,128]{2,1,0:T(8,128)S(1)}, f32[12,8,128]{2,1,0:T(8,128)S(1)}, u32[]{:S(2)}, u32[]{:S(2)}) collective-permute-start(f32[12,8,128]{2,1,0:T(8,128)S(1)} %bitcast_add_fusion), channel_id=1, source_target_pairs={{0,64},{64,128},{128,192},{192,0},{1,65},{65,129},{129,193},{193,1... | collective-permute-start | bytes 147464 | tf_op jit(solution)/shard_map/ppermute | solution.py:195
  13.1 15.9 %collective-permute-start.9 = (f32[23,32,128]{2,1,0:T(8,128)S(1)}, f32[23,32,128]{2,1,0:T(8,128)S(1)}, u32[]{:S(2)}, u32[]{:S(2)}) collective-permute-start(f32[23,32,128]{2,1,0:T(8,128)S(1)} %get-tuple-element.13), channel_id=1, source_target_pairs={{0,3},{1,0},{2,1},{3,2},{4,7},{5,4},{6,5},{7,6},{8,11},{9,8},{10,9... | collective-permute-start | bytes 1130504 | tf_op jit(solution)/shard_map/ppermute | solution.py:195
  15.5 13.5 %collective-permute-start.10 = (f32[23,32,128]{2,1,0:T(8,128)S(1)}, f32[23,32,128]{2,1,0:T(8,128)S(1)}, u32[]{:S(2)}, u32[]{:S(2)}) collective-permute-start(f32[23,32,128]{2,1,0:T(8,128)S(1)} %get-tuple-element.15), channel_id=1, source_target_pairs={{0,1},{1,2},{2,3},{3,0},{4,5},{5,6},{6,7},{7,4},{8,9},{9,10},{10,1... | collective-permute-start | bytes 1130504 | tf_op jit(solution)/shard_map/ppermute | solution.py:195
  17.0 7.4 %collective-permute-start.5 = (f32[12,8,128]{2,1,0:T(8,128)S(1)}, f32[12,8,128]{2,1,0:T(8,128)S(1)}, u32[]{:S(2)}, u32[]{:S(2)}) collective-permute-start(f32[12,8,128]{2,1,0:T(8,128)S(1)} %add_add_fusion.1), channel_id=1, source_target_pairs={{0,8},{8,16},{16,24},{24,32},{32,40},{40,48},{48,56},{56,0},{1,9},... | collective-permute-start | bytes 147464 | tf_op jit(solution)/shard_map/ppermute | solution.py:195
  18.7 5.7 %collective-permute-start.4 = (f32[12,8,128]{2,1,0:T(8,128)S(1)}, f32[12,8,128]{2,1,0:T(8,128)S(1)}, u32[]{:S(2)}, u32[]{:S(2)}) collective-permute-start(f32[12,8,128]{2,1,0:T(8,128)S(1)} %add_add_fusion.1), channel_id=1, source_target_pairs={{0,56},{8,0},{16,8},{24,16},{32,24},{40,32},{48,40},{56,48},{1,57}... | collective-permute-start | bytes 147464 | tf_op jit(solution)/shard_map/ppermute | solution.py:195
  24.4 7.4 %collective-permute-start.7 = (f32[12,8,128]{2,1,0:T(8,128)S(1)}, f32[12,8,128]{2,1,0:T(8,128)S(1)}, u32[]{:S(2)}, u32[]{:S(2)}) collective-permute-start(f32[12,8,128]{2,1,0:T(8,128)S(1)} %get-tuple-element.18), channel_id=1, source_target_pairs={{0,24},{8,32},{16,40},{24,48},{32,56},{40,0},{48,8},{56,16},{1,25}... | collective-permute-start | bytes 147464 | tf_op jit(solution)/shard_map/ppermute | solution.py:195
  28.8 4.8 %collective-permute-start.6 = (f32[12,8,128]{2,1,0:T(8,128)S(1)}, f32[12,8,128]{2,1,0:T(8,128)S(1)}, u32[]{:S(2)}, u32[]{:S(2)}) collective-permute-start(f32[12,8,128]{2,1,0:T(8,128)S(1)} %get-tuple-element.17), channel_id=1, source_target_pairs={{0,40},{8,48},{16,56},{24,0},{32,8},{40,16},{48,24},{56,32},{1,41}... | collective-permute-start | bytes 147464 | tf_op jit(solution)/shard_map/ppermute | solution.py:195
  29.1 10.8 %collective-permute-start.11 = (f32[23,16,128]{2,1,0:T(8,128)S(1)}, f32[23,16,128]{2,1,0:T(8,128)S(1)}, u32[]{:S(2)}, u32[]{:S(2)}) collective-permute-start(f32[23,16,128]{2,1,0:T(8,128)S(1)} %get-tuple-element.21), channel_id=1, source_target_pairs={{0,1},{1,2},{2,3},{3,0},{4,5},{5,6},{6,7},{7,4},{8,9},{9,10},{10,1... | collective-permute-start | bytes 565256 | tf_op jit(solution)/shard_map/ppermute | solution.py:195
  30.1 9.8 %collective-permute-start.12 = (f32[23,16,128]{2,1,0:T(8,128)S(1)}, f32[23,16,128]{2,1,0:T(8,128)S(1)}, u32[]{:S(2)}, u32[]{:S(2)}) collective-permute-start(f32[23,16,128]{2,1,0:T(8,128)S(1)} %get-tuple-element.22), channel_id=1, source_target_pairs={{0,3},{1,0},{2,1},{3,2},{4,7},{5,4},{6,5},{7,6},{8,11},{9,8},{10,9... | collective-permute-start | bytes 565256 | tf_op jit(solution)/shard_map/ppermute | solution.py:195
  33.7 5.2 %collective-permute-start.8 = (f32[12,8,128]{2,1,0:T(8,128)S(1)}, f32[12,8,128]{2,1,0:T(8,128)S(1)}, u32[]{:S(2)}, u32[]{:S(2)}) collective-permute-start(f32[12,8,128]{2,1,0:T(8,128)S(1)} %add_add_fusion.mine_ref), channel_id=1, source_target_pairs={{0,4},{4,0},{1,5},{5,1},{2,6},{6,2},{3,7},{7,3},{8,12},{12,8},{9,1... | collective-permute-start | bytes 147464 | tf_op jit(solution)/shard_map/ppermute | solution.py:195

commit v4 on v3

--- a/solution.py
+++ b/solution.py
@@ -9,7 +9,7 @@
 REGIONS = 46
 HALF = 64
 PARTS = 4
-SLOTS = 24
+ROWS = 48
 TILES = 16
 CHUNK = 8
 CELL_AXES = ("y", "z", "core")
@@ -103,22 +103,21 @@
         acc_ref[...] += part
 
 
-def packed_sums(acc_ref, sums_ref, days_in):
-    group = sums_ref.shape[1]
-    members = group // 2
+def packed_sums(acc_ref, sums_ref, days_in, members):
+    group = 2 * members
     days = days_in - WINDOW + 1
+    columns = sums_ref.shape[1] // members
     v = acc_ref[: (days_in + 2) * group].reshape(days_in + 2, group, 2 * HALF)
     pair = v[: days_in - 1] + v[1:days_in]
     rolled = (pair[0:days] + pair[2 : 2 + days] + pair[4 : 4 + days]) * (1.0 / WINDOW)
-    pad = jnp.zeros((4 * SLOTS - days - 2, group, 2 * HALF), jnp.float32)
-    v = jnp.concatenate([rolled, v[days_in:], pad], axis=0)
-    s = v + pltpu.roll(pltpu.roll(v, members, 1), HALF, 2)
-    r = pltpu.roll(s, HALF, 2)
-    top = lax.broadcasted_iota(jnp.int32, (SLOTS, group, 2 * HALF), 1) < members
-    low = lax.broadcasted_iota(jnp.int32, (SLOTS, group, 2 * HALF), 2) < HALF
-    upper = jnp.where(low, s[0:SLOTS], r[SLOTS : 2 * SLOTS])
-    lower = jnp.where(low, r[2 * SLOTS : 3 * SLOTS], s[3 * SLOTS :])
-    sums_ref[...] = jnp.where(top, upper, lower)
+    acc_ref[: days * group] = rolled.reshape(days * group, 2 * HALF)
+    acc_ref[days * group : (days + 2) * group] = v[days_in:].reshape(2 * group, 2 * HALF)
+    rows = []
+    for m in range(members):
+        even = acc_ref[pl.ds(m, columns, stride=group), :]
+        odd = acc_ref[pl.ds(members + m, columns, stride=group), :]
+        rows.append(even + pltpu.roll(odd, HALF, 1))
+    sums_ref[...] = jnp.concatenate(rows, axis=0).T[: sums_ref.shape[0]]
 
 
 def fold_kernel(fill_ref, x_ref, thr_ref, mask_ref, rid_ref, area_ref, *refs):
@@ -132,27 +131,22 @@
 
     @pl.when(step == pl.num_programs(0) - 1)
     def _():
-        packed_sums(acc_ref, sums_ref, x_ref.shape[0])
-
-
-def table_kernel(mine_ref, other_ref, index_ref, count_ref, rows_ref):
-    half, group, lanes = mine_ref.shape
-    members = group // 2
-    days = index_ref.shape[2]
-    core = lax.axis_index("core")
-    mine = mine_ref[...].reshape(half * group, lanes)
-    other = other_ref[...].reshape(half * group, lanes)
-    rows_ref[: half * group] = jnp.where(core == 0, mine, other)
-    rows_ref[half * group :] = jnp.where(core == 0, other, mine)
+        packed_sums(acc_ref, sums_ref, x_ref.shape[0], x_ref.shape[1] // live.shape[0])
+
+
+def table_kernel(mine_ref, other_ref, index_ref, count_ref):
+    members, days = index_ref.shape[1:]
+    width = mine_ref.shape[1]
+    columns = width // members
+    first = lax.axis_index("core") == 0
+    mine, other = mine_ref[...], other_ref[...]
+    table = jnp.concatenate([jnp.where(first, mine, other), jnp.where(first, other, mine)], axis=0)
+    count = jnp.broadcast_to(table[:, days + 1 : days + 2], (table.shape[0], 128)).T
+    count_ref[...] = count[:1, :REGIONS].astype(jnp.int32)
+    table = table / table[:, days : days + 1]
     for m in range(members):
-        upper = rows_ref[pl.ds(m, 2 * half, stride=group), :]
-        lower = rows_ref[pl.ds(members + m, 2 * half, stride=group), :]
-        rows = [upper, pltpu.roll(upper, HALF, 1), lower, pltpu.roll(lower, HALF, 1)]
-        table = jnp.concatenate(rows, axis=0)
-        if m == 0:
-            count_ref[...] = table[days + 1 : days + 2, :REGIONS].astype(jnp.int32)
-        by_region = table.T[:REGIONS]
-        index_ref[:, m, :] = by_region[:, :days] / by_region[:, days : days + 1]
+        shifted = pltpu.roll(table, (width - m * columns) % width, 1) if m else table
+        index_ref[:, m, :] = shifted[:REGIONS, :days]
 
 
 def call(kernel, fill, x, flats, blocks, regional):
@@ -165,8 +159,9 @@
     out_shape = [jax.ShapeDtypeStruct((block_days, tiles, lanes), jnp.float32)] * blocks
     scratch = []
     if regional:
-        sums = (SLOTS, 2 * members, 2 * HALF)
-        out_specs.append(pl.BlockSpec(sums, lambda i: (0, 0, 0)))
+        columns = -(-(days_in - WINDOW + 3) // 8) * 8
+        sums = (ROWS, members * columns)
+        out_specs.append(pl.BlockSpec(sums, lambda i: (0, 0)))
         out_shape.append(jax.ShapeDtypeStruct(sums, jnp.float32))
         high = -(-(days_in + 2) * 2 * members // 16) * 16
         scratch = [
@@ -235,13 +230,13 @@
     first, second = sum_over_members(*terms)
     mine, other = sum_over_cells(sums)
     cell_mean = jnp.concatenate([first, second], axis=1).reshape(-1, cells)
+    other, cell_mean = lax.optimization_barrier((other, cell_mean))
     region_index, land_count = pl.pallas_call(
         table_kernel,
         out_shape=[
             jax.ShapeDtypeStruct((REGIONS, members, days), jnp.float32),
             jax.ShapeDtypeStruct((1, REGIONS), jnp.int32),
         ],
-        scratch_shapes=[pltpu.VMEM((SLOTS * 2 * members, 2 * HALF), jnp.float32)],
         compiler_params=pltpu.CompilerParams(vmem_limit_bytes=4 * 1024 * 1024),
     )(mine, other)
     return region_index.transpose(1, 2, 0), cell_mean, land_count.reshape(REGIONS)

time: 41.1 us -> 39.6 us (0.964)
  waiting for transfers between devices: 6.75 us -> 5.32 us
    ppermute x13, waiting for transfers between devices: 6.75 us -> 5.32 us  [moved(): lax.ppermute(array, axis, [(i, (i + shift) % size) for i in range(size)])]
  transfers between devices with their start and end apart: 13 -> 13, of which waited for: 6 -> 5; matrix products, arithmetic and copies ran while one was open for 0% -> 3% of each run, Pallas kernels for 2% -> 0%
where the time goes in v4:
time: 39.6 us; the launch traced here: 39.4 us
  starting transfers between devices  25.2 us (64%)
  Pallas kernels  6.96 us (18%)
  waiting for transfers between devices  5.32 us (13%)
  local copies, waits for them, and re-layouts  1.02 us (3%)
  between operations  0.7 us (2%)
    ppermute x13, starting transfers between devices, moved(): lax.ppermute(array, axis, [(i, (i + shift) % size) for i in range(size)])  25.2 us
    pallas_call x1, Pallas kernels, call(): pl.pallas_call(kernel, grid=(tiles // TILES,), in_specs=[pl.BlockSpec(fil...  6.11 us
    ppermute x13, waiting for transfers between devices, moved(): lax.ppermute(array, axis, [(i, (i + shift) % size) for i in range(size)])  5.32 us
    unnamed x2, local copies, waits for them, and re-layouts  1.01 us
    pallas_call x1, Pallas kernels, shards(): pl.pallas_call(table_kernel, out_shape=[jax.ShapeDtypeStruct((REGIONS, me...  0.86 us
  transfers between devices with their start and end apart: 13, of which 5 were waited for; matrix products, arithmetic and copies ran while one was open for 3% of the time, Pallas kernels for 0%

profile of v4, /device:TPU:1, one launch (start us, length us, event | category | flops | bytes accessed | tf_op | source)
XLA Modules:
  0.0 39.4 jit_solution(17947958511289887649)
XLA Ops:
  0.6 6.1 %shard_map.85 = (f32[23,32,128]{2,1,0:T(8,128)S(1)}, f32[23,32,128]{2,1,0:T(8,128)S(1)}, f32[23,32,128]{2,1,0:T(8,128)S(1)}, f32[23,32,128]{2,1,0:T(8,128)S(1)}, f32[48,384]{1,0:T(8,128)S(1)}) custom-call(s32[1,32]{1,0:T(1,128)} %bitcast.29, f32[97,128,128]{2,1,0:T(8,128)} %bitcast.22, s32[32,128]{1,0:T(8,128)} %bitcast.25, s32[32,128]{1,0:T(8,128)} %bitcast.26, ...), custom_call_target="tpu_custom_call" | custom-call | tf_op jit(solution)/shard_map/pallas_call | solution.py:173
  6.8 3.3 %collective-permute-start = (f32[24,384]{1,0:T(8,128)S(1)}, f32[24,384]{1,0:T(8,128)S(1)}, u32[]{:S(2)}, u32[]{:S(2)}) collective-permute-start(f32[24,384]{1,0:T(8,128)S(1)} %dynamic-slice_bitcast_fusion), channel_id=1, source_target_pairs={{0,4},{4,0},{1,5},{5,1},{2,6},{6,2},{3,7},{7,3},{8,12},{12,8},{9,1... | collective-permute-start | bytes 110600 | tf_op jit(solution)/shard_map/ppermute | solution.py:190
  10.1 0.9 %collective-permute-done = f32[24,384]{1,0:T(8,128)S(1)} collective-permute-done((f32[24,384]{1,0:T(8,128)S(1)}, f32[24,384]{1,0:T(8,128)S(1)}, u32[]{:S(2)}, u32[]{:S(2)}) %collective-permute-start) | collective-permute-done | bytes 36896 | tf_op jit(solution)/shard_map/ppermute | solution.py:190
  11.0 1.0 %collective-permute-start.3 = (f32[24,384]{1,0:T(8,128)S(1)}, f32[24,384]{1,0:T(8,128)S(1)}, u32[]{:S(2)}, u32[]{:S(2)}) collective-permute-start(f32[24,384]{1,0:T(8,128)S(1)} %bitcast_add_fusion), channel_id=1, source_target_pairs={{0,192},{64,0},{128,64},{192,128},{1,193},{65,1},{129,65},{193,129... | collective-permute-start | bytes 110600 | tf_op jit(solution)/shard_map/ppermute | solution.py:190
  12.0 0.4 collective-permute-start.2
  12.3 0.7 %collective-permute-start.1 = (f32[24,384]{1,0:T(8,128)S(1)}, f32[24,384]{1,0:T(8,128)S(1)}, u32[]{:S(2)}, u32[]{:S(2)}) collective-permute-start(f32[24,384]{1,0:T(8,128)S(1)} %bitcast_add_fusion), channel_id=1, source_target_pairs={{0,64},{64,128},{128,192},{192,0},{1,65},{65,129},{129,193},{193,1... | collective-permute-start | bytes 110600 | tf_op jit(solution)/shard_map/ppermute | solution.py:190
  13.0 2.5 %collective-permute-start.9 = (f32[23,32,128]{2,1,0:T(8,128)S(1)}, f32[23,32,128]{2,1,0:T(8,128)S(1)}, u32[]{:S(2)}, u32[]{:S(2)}) collective-permute-start(f32[23,32,128]{2,1,0:T(8,128)S(1)} %get-tuple-element.14), channel_id=1, source_target_pairs={{0,3},{1,0},{2,1},{3,2},{4,7},{5,4},{6,5},{7,6},{8,11},{9,8},{10,9... | collective-permute-start | bytes 1130504 | tf_op jit(solution)/shard_map/ppermute | solution.py:190
  15.5 0.0 collective-permute-start.10
  15.5 0.0 collective-permute-done.3
  15.5 0.8 %collective-permute-done.2 = f32[24,384]{1,0:T(8,128)S(1)} collective-permute-done((f32[24,384]{1,0:T(8,128)S(1)}, f32[24,384]{1,0:T(8,128)S(1)}, u32[]{:S(2)}, u32[]{:S(2)}) %collective-permute-start.2) | collective-permute-done | bytes 36896 | tf_op jit(solution)/shard_map/ppermute | solution.py:190
  16.3 0.4 collective-permute-done.1
  16.7 1.7 %collective-permute-start.5 = (f32[24,384]{1,0:T(8,128)S(1)}, f32[24,384]{1,0:T(8,128)S(1)}, u32[]{:S(2)}, u32[]{:S(2)}) collective-permute-start(f32[24,384]{1,0:T(8,128)S(1)} %add_add_fusion.1), channel_id=1, source_target_pairs={{0,8},{8,16},{16,24},{24,32},{32,40},{40,48},{48,56},{56,0},{1,9},... | collective-permute-start | bytes 110600 | tf_op jit(solution)/shard_map/ppermute | solution.py:190
  18.4 4.0 %collective-permute-start.4 = (f32[24,384]{1,0:T(8,128)S(1)}, f32[24,384]{1,0:T(8,128)S(1)}, u32[]{:S(2)}, u32[]{:S(2)}) collective-permute-start(f32[24,384]{1,0:T(8,128)S(1)} %add_add_fusion.1), channel_id=1, source_target_pairs={{0,56},{8,0},{16,8},{24,16},{32,24},{40,32},{48,40},{56,48},{1,57}... | collective-permute-start | bytes 110600 | tf_op jit(solution)/shard_map/ppermute | solution.py:190
  22.4 1.6 %collective-permute-done.5 = f32[24,384]{1,0:T(8,128)S(1)} collective-permute-done((f32[24,384]{1,0:T(8,128)S(1)}, f32[24,384]{1,0:T(8,128)S(1)}, u32[]{:S(2)}, u32[]{:S(2)}) %collective-permute-start.5) | collective-permute-done | bytes 36896 | tf_op jit(solution)/shard_map/ppermute | solution.py:190
  24.0 0.0 collective-permute-done.4
  24.0 4.4 %collective-permute-start.7 = (f32[24,384]{1,0:T(8,128)S(1)}, f32[24,384]{1,0:T(8,128)S(1)}, u32[]{:S(2)}, u32[]{:S(2)}) collective-permute-start(f32[24,384]{1,0:T(8,128)S(1)} %get-tuple-element.22), channel_id=1, source_target_pairs={{0,24},{8,32},{16,40},{24,48},{32,56},{40,0},{48,8},{56,16},{1,25}... | collective-permute-start | bytes 110600 | tf_op jit(solution)/shard_map/ppermute | solution.py:190
  28.4 0.2 collective-permute-start.6
  28.6 0.0 collective-permute-done.9
  28.6 0.0 collective-permute-done.10
  28.6 0.1 slice_add_fusion.2
  28.6 1.0 %collective-permute-start.11 = (f32[23,16,128]{2,1,0:T(8,128)S(1)}, f32[23,16,128]{2,1,0:T(8,128)S(1)}, u32[]{:S(2)}, u32[]{:S(2)}) collective-permute-start(f32[23,16,128]{2,1,0:T(8,128)S(1)} %get-tuple-element.25), channel_id=1, source_target_pairs={{0,1},{1,2},{2,3},{3,0},{4,5},{5,6},{6,7},{7,4},{8,9},{9,10},{10,1... | collective-permute-start | bytes 565256 | tf_op jit(solution)/shard_map/ppermute | solution.py:190
  29.6 1.8 %collective-permute-start.12 = (f32[23,16,128]{2,1,0:T(8,128)S(1)}, f32[23,16,128]{2,1,0:T(8,128)S(1)}, u32[]{:S(2)}, u32[]{:S(2)}) collective-permute-start(f32[23,16,128]{2,1,0:T(8,128)S(1)} %get-tuple-element.26), channel_id=1, source_target_pairs={{0,3},{1,0},{2,1},{3,2},{4,7},{5,4},{6,5},{7,6},{8,11},{9,8},{10,9... | collective-permute-start | bytes 565256 | tf_op jit(solution)/shard_map/ppermute | solution.py:190
  31.4 0.0 collective-permute-done.7
  31.4 1.7 %collective-permute-done.6 = f32[24,384]{1,0:T(8,128)S(1)} collective-permute-done((f32[24,384]{1,0:T(8,128)S(1)}, f32[24,384]{1,0:T(8,128)S(1)}, u32[]{:S(2)}, u32[]{:S(2)}) %collective-permute-start.6) | collective-permute-done | bytes 36896 | tf_op jit(solution)/shard_map/ppermute | solution.py:190
  33.1 4.3 %collective-permute-start.8 = (f32[24,384]{1,0:T(8,128)S(1)}, f32[24,384]{1,0:T(8,128)S(1)}, u32[]{:S(2)}, u32[]{:S(2)}) collective-permute-start(f32[24,384]{1,0:T(8,128)S(1)} %add_add_fusion.mine_ref), channel_id=1, source_target_pairs={{0,4},{4,0},{1,5},{5,1},{2,6},{6,2},{3,7},{7,3},{8,12},{12,8},{9,1... | collective-permute-start | bytes 110600 | tf_op jit(solution)/shard_map/ppermute | solution.py:190
  37.4 0.0 collective-permute-done.11
  37.4 0.0 collective-permute-done.12
  37.4 0.1 fusion.1
  37.6 1.0 %copy.10 = f32[3,8,32,128]{3,1,2,0:T(8,128)} copy(f32[3,8,32,128]{3,2,1,0:T(8,128)S(1)} %bitcast.23) | data formatting | bytes 786432
  38.6 0.0 collective-permute-done.8.other_ref
  38.6 0.9 %shard_map.86 = (f32[46,4,92]{2,1,0:T(4,128)}, s32[1,46]{1,0:T(1,128)}) custom-call(f32[24,384]{1,0:T(8,128)S(1)} %add_add_fusion.mine_ref, f32[24,384]{1,0:T(8,128)S(1)} %collective-permute-done.8.other_ref), custom_call_target="tpu_custom_call" | custom-call | tf_op jit(solution)/shard_map/pallas_call | solution.py:234
  (7 shorter events, 0.1 us)
Async XLA Ops:
  6.8 4.2 %collective-permute-start = (f32[24,384]{1,0:T(8,128)S(1)}, f32[24,384]{1,0:T(8,128)S(1)}, u32[]{:S(2)}, u32[]{:S(2)}) collective-permute-start(f32[24,384]{1,0:T(8,128)S(1)} %dynamic-slice_bitcast_fusion), channel_id=1, source_target_pairs={{0,4},{4,0},{1,5},{5,1},{2,6},{6,2},{3,7},{7,3},{8,12},{12,8},{9,1... | collective-permute-start | bytes 110600 | tf_op jit(solution)/shard_map/ppermute | solution.py:190
  11.0 4.5 %collective-permute-start.3 = (f32[24,384]{1,0:T(8,128)S(1)}, f32[24,384]{1,0:T(8,128)S(1)}, u32[]{:S(2)}, u32[]{:S(2)}) collective-permute-start(f32[24,384]{1,0:T(8,128)S(1)} %bitcast_add_fusion), channel_id=1, source_target_pairs={{0,192},{64,0},{128,64},{192,128},{1,193},{65,1},{129,65},{193,129... | collective-permute-start | bytes 110600 | tf_op jit(solution)/shard_map/ppermute | solution.py:190
  12.0 4.3 %collective-permute-start.2 = (f32[24,384]{1,0:T(8,128)S(1)}, f32[24,384]{1,0:T(8,128)S(1)}, u32[]{:S(2)}, u32[]{:S(2)}) collective-permute-start(f32[24,384]{1,0:T(8,128)S(1)} %bitcast_add_fusion), channel_id=1, source_target_pairs={{0,128},{64,192},{128,0},{192,64},{1,129},{65,193},{129,1},{193,65... | collective-permute-start | bytes 110600 | tf_op jit(solution)/shard_map/ppermute | solution.py:190
  12.3 4.4 %collective-permute-start.1 = (f32[24,384]{1,0:T(8,128)S(1)}, f32[24,384]{1,0:T(8,128)S(1)}, u32[]{:S(2)}, u32[]{:S(2)}) collective-permute-start(f32[24,384]{1,0:T(8,128)S(1)} %bitcast_add_fusion), channel_id=1, source_target_pairs={{0,64},{64,128},{128,192},{192,0},{1,65},{65,129},{129,193},{193,1... | collective-permute-start | bytes 110600 | tf_op jit(solution)/shard_map/ppermute | solution.py:190
  13.0 15.6 %collective-permute-start.9 = (f32[23,32,128]{2,1,0:T(8,128)S(1)}, f32[23,32,128]{2,1,0:T(8,128)S(1)}, u32[]{:S(2)}, u32[]{:S(2)}) collective-permute-start(f32[23,32,128]{2,1,0:T(8,128)S(1)} %get-tuple-element.14), channel_id=1, source_target_pairs={{0,3},{1,0},{2,1},{3,2},{4,7},{5,4},{6,5},{7,6},{8,11},{9,8},{10,9... | collective-permute-start | bytes 1130504 | tf_op jit(solution)/shard_map/ppermute | solution.py:190
  15.5 13.1 %collective-permute-start.10 = (f32[23,32,128]{2,1,0:T(8,128)S(1)}, f32[23,32,128]{2,1,0:T(8,128)S(1)}, u32[]{:S(2)}, u32[]{:S(2)}) collective-permute-start(f32[23,32,128]{2,1,0:T(8,128)S(1)} %get-tuple-element.16), channel_id=1, source_target_pairs={{0,1},{1,2},{2,3},{3,0},{4,5},{5,6},{6,7},{7,4},{8,9},{9,10},{10,1... | collective-permute-start | bytes 1130504 | tf_op jit(solution)/shard_map/ppermute | solution.py:190
  16.7 7.3 %collective-permute-start.5 = (f32[24,384]{1,0:T(8,128)S(1)}, f32[24,384]{1,0:T(8,128)S(1)}, u32[]{:S(2)}, u32[]{:S(2)}) collective-permute-start(f32[24,384]{1,0:T(8,128)S(1)} %add_add_fusion.1), channel_id=1, source_target_pairs={{0,8},{8,16},{16,24},{24,32},{32,40},{40,48},{48,56},{56,0},{1,9},... | collective-permute-start | bytes 110600 | tf_op jit(solution)/shard_map/ppermute | solution.py:190
  18.4 5.6 %collective-permute-start.4 = (f32[24,384]{1,0:T(8,128)S(1)}, f32[24,384]{1,0:T(8,128)S(1)}, u32[]{:S(2)}, u32[]{:S(2)}) collective-permute-start(f32[24,384]{1,0:T(8,128)S(1)} %add_add_fusion.1), channel_id=1, source_target_pairs={{0,56},{8,0},{16,8},{24,16},{32,24},{40,32},{48,40},{56,48},{1,57}... | collective-permute-start | bytes 110600 | tf_op jit(solution)/shard_map/ppermute | solution.py:190
  24.0 7.4 %collective-permute-start.7 = (f32[24,384]{1,0:T(8,128)S(1)}, f32[24,384]{1,0:T(8,128)S(1)}, u32[]{:S(2)}, u32[]{:S(2)}) collective-permute-start(f32[24,384]{1,0:T(8,128)S(1)} %get-tuple-element.22), channel_id=1, source_target_pairs={{0,24},{8,32},{16,40},{24,48},{32,56},{40,0},{48,8},{56,16},{1,25}... | collective-permute-start | bytes 110600 | tf_op jit(solution)/shard_map/ppermute | solution.py:190
  28.4 4.7 %collective-permute-start.6 = (f32[24,384]{1,0:T(8,128)S(1)}, f32[24,384]{1,0:T(8,128)S(1)}, u32[]{:S(2)}, u32[]{:S(2)}) collective-permute-start(f32[24,384]{1,0:T(8,128)S(1)} %get-tuple-element.21), channel_id=1, source_target_pairs={{0,40},{8,48},{16,56},{24,0},{32,8},{40,16},{48,24},{56,32},{1,41}... | collective-permute-start | bytes 110600 | tf_op jit(solution)/shard_map/ppermute | solution.py:190
  28.6 8.8 %collective-permute-start.11 = (f32[23,16,128]{2,1,0:T(8,128)S(1)}, f32[23,16,128]{2,1,0:T(8,128)S(1)}, u32[]{:S(2)}, u32[]{:S(2)}) collective-permute-start(f32[23,16,128]{2,1,0:T(8,128)S(1)} %get-tuple-element.25), channel_id=1, source_target_pairs={{0,1},{1,2},{2,3},{3,0},{4,5},{5,6},{6,7},{7,4},{8,9},{9,10},{10,1... | collective-permute-start | bytes 565256 | tf_op jit(solution)/shard_map/ppermute | solution.py:190
  29.6 7.8 %collective-permute-start.12 = (f32[23,16,128]{2,1,0:T(8,128)S(1)}, f32[23,16,128]{2,1,0:T(8,128)S(1)}, u32[]{:S(2)}, u32[]{:S(2)}) collective-permute-start(f32[23,16,128]{2,1,0:T(8,128)S(1)} %get-tuple-element.26), channel_id=1, source_target_pairs={{0,3},{1,0},{2,1},{3,2},{4,7},{5,4},{6,5},{7,6},{8,11},{9,8},{10,9... | collective-permute-start | bytes 565256 | tf_op jit(solution)/shard_map/ppermute | solution.py:190
  33.1 5.5 %collective-permute-start.8 = (f32[24,384]{1,0:T(8,128)S(1)}, f32[24,384]{1,0:T(8,128)S(1)}, u32[]{:S(2)}, u32[]{:S(2)}) collective-permute-start(f32[24,384]{1,0:T(8,128)S(1)} %add_add_fusion.mine_ref), channel_id=1, source_target_pairs={{0,4},{4,0},{1,5},{5,1},{2,6},{6,2},{3,7},{7,3},{8,12},{12,8},{9,1... | collective-permute-start | bytes 110600 | tf_op jit(solution)/shard_map/ppermute | solution.py:190

commit v5 on v4

--- a/solution.py
+++ b/solution.py
@@ -134,7 +134,23 @@
         packed_sums(acc_ref, sums_ref, x_ref.shape[0], x_ref.shape[1] // live.shape[0])
 
 
-def table_kernel(mine_ref, other_ref, index_ref, count_ref):
+def last_kernel(
+    mine_ref, other_ref, own_ref, below_ref, above_ref, far_ref, near_ref,
+    index_ref, count_ref, mean_ref, total_ref,
+):
+    block_days, tiles, lanes = own_ref.shape
+    cut = tiles // 2
+    first = own_ref[:, :cut] + above_ref[:, :cut] + near_ref[...]
+    second = own_ref[:, cut:] + below_ref[:, cut:] + far_ref[...]
+    total_ref[: block_days * cut] = first.reshape(block_days * cut, lanes)
+    total_ref[block_days * cut :] = second.reshape(block_days * cut, lanes)
+    for t in range(tiles):
+        rows = pl.ds(t // cut * block_days * cut + t % cut, block_days, stride=cut)
+        mean_ref[:, t * lanes : (t + 1) * lanes] = total_ref[rows, :]
+    region_table(mine_ref, other_ref, index_ref, count_ref)
+
+
+def region_table(mine_ref, other_ref, index_ref, count_ref):
     members, days = index_ref.shape[1:]
     width = mine_ref.shape[1]
     columns = width // members
@@ -204,14 +220,11 @@
 
 
 def sum_over_members(own, up, down, late):
-    tiles = own.shape[1]
-    cut = tiles // 2
+    cut = own.shape[1] // 2
     from_below, from_above = moved(up, "x", 1), moved(down, "x", 3)
     near = moved(late[:, :cut] + from_below[:, :cut], "x", 1)
     far = moved(late[:, cut:] + from_above[:, cut:], "x", 3)
-    first = own[:, :cut] + from_above[:, :cut] + near
-    second = own[:, cut:] + from_below[:, cut:] + far
-    return first, second
+    return own, from_below, from_above, far, near
 
 
 def shards(tmax, threshold, land_mask, region_id, block_fill, cell_area):
@@ -227,18 +240,19 @@
     *terms, sums = call(
         fold_kernel, block_fill.reshape(1, blocks), x, (threshold, land_mask, region_id, cell_area), PARTS, True
     )
-    first, second = sum_over_members(*terms)
+    terms = sum_over_members(*terms)
     mine, other = sum_over_cells(sums)
-    cell_mean = jnp.concatenate([first, second], axis=1).reshape(-1, cells)
-    other, cell_mean = lax.optimization_barrier((other, cell_mean))
-    region_index, land_count = pl.pallas_call(
-        table_kernel,
+    block_days = terms[0].shape[0]
+    region_index, land_count, cell_mean = pl.pallas_call(
+        last_kernel,
         out_shape=[
             jax.ShapeDtypeStruct((REGIONS, members, days), jnp.float32),
             jax.ShapeDtypeStruct((1, REGIONS), jnp.int32),
+            jax.ShapeDtypeStruct((block_days, cells), jnp.float32),
         ],
-        compiler_params=pltpu.CompilerParams(vmem_limit_bytes=4 * 1024 * 1024),
-    )(mine, other)
+        scratch_shapes=[pltpu.VMEM((block_days * blocks, lanes), jnp.float32)],
+        compiler_params=pltpu.CompilerParams(vmem_limit_bytes=8 * 1024 * 1024),
+    )(mine, other, *terms)
     return region_index.transpose(1, 2, 0), cell_mean, land_count.reshape(REGIONS)
 
 

time: 39.6 us -> 39.5 us (level)
  local copies, waits for them, and re-layouts: 1.02 us -> 0.01 us
  waiting for transfers between devices: 5.32 us -> 5.98 us
    unnamed x2 -> x0, local copies, waits for them, and re-layouts: 1.01 us -> none
    ppermute x13, waiting for transfers between devices: 5.32 us -> 5.98 us  [moved(): lax.ppermute(array, axis, [(i, (i + shift) % size) for i in range(size)])]
  transfers between devices with their start and end apart: 13 -> 13, of which waited for: 5 -> 6; matrix products, arithmetic and copies ran while one was open for 3% -> 0% of each run, Pallas kernels for 0% -> 0%
where the time goes in v5:
time: 39.5 us; the launch traced here: 39.4 us
  starting transfers between devices  25.4 us (64%)
  Pallas kernels  7.22 us (18%)
  waiting for transfers between devices  5.98 us (15%)
  between operations  0.68 us (2%)
    ppermute x13, starting transfers between devices, moved(): lax.ppermute(array, axis, [(i, (i + shift) % size) for i in range(size)])  25.4 us
    pallas_call x1, Pallas kernels, call(): pl.pallas_call(kernel, grid=(tiles // TILES,), in_specs=[pl.BlockSpec(fil...  6.11 us
    ppermute x13, waiting for transfers between devices, moved(): lax.ppermute(array, axis, [(i, (i + shift) % size) for i in range(size)])  5.98 us
    pallas_call x1, Pallas kernels, shards(): pl.pallas_call(last_kernel, out_shape=[jax.ShapeDtypeStruct((REGIONS, mem...  1.11 us
  transfers between devices with their start and end apart: 13, of which 6 were waited for; matrix products, arithmetic and copies ran while one was open for 0% of the time, Pallas kernels for 0%

profile of v5, /device:TPU:1, one launch (start us, length us, event | category | flops | bytes accessed | tf_op | source)
XLA Modules:
  0.0 39.4 jit_solution(10809519580032449970)
XLA Ops:
  0.6 6.1 %shard_map.85 = (f32[23,32,128]{2,1,0:T(8,128)S(1)}, f32[23,32,128]{2,1,0:T(8,128)S(1)}, f32[23,32,128]{2,1,0:T(8,128)S(1)}, f32[23,32,128]{2,1,0:T(8,128)S(1)}, f32[48,384]{1,0:T(8,128)S(1)}) custom-call(s32[1,32]{1,0:T(1,128)} %bitcast.24, f32[97,128,128]{2,1,0:T(8,128)} %bitcast.19, s32[32,128]{1,0:T(8,128)} %bitcast.20, s32[32,128]{1,0:T(8,128)} %bitcast.21, ...), custom_call_target="tpu_custom_call" | custom-call | tf_op jit(solution)/shard_map/pallas_call | solution.py:189
  6.8 3.3 %collective-permute-start = (f32[24,384]{1,0:T(8,128)S(1)}, f32[24,384]{1,0:T(8,128)S(1)}, u32[]{:S(2)}, u32[]{:S(2)}) collective-permute-start(f32[24,384]{1,0:T(8,128)S(1)} %dynamic-slice_bitcast_fusion), channel_id=1, source_target_pairs={{0,4},{4,0},{1,5},{5,1},{2,6},{6,2},{3,7},{7,3},{8,12},{12,8},{9,1... | collective-permute-start | bytes 110600 | tf_op jit(solution)/shard_map/ppermute | solution.py:206
  10.1 0.9 %collective-permute-done = f32[24,384]{1,0:T(8,128)S(1)} collective-permute-done((f32[24,384]{1,0:T(8,128)S(1)}, f32[24,384]{1,0:T(8,128)S(1)}, u32[]{:S(2)}, u32[]{:S(2)}) %collective-permute-start) | collective-permute-done | bytes 36896 | tf_op jit(solution)/shard_map/ppermute | solution.py:206
  11.0 1.0 %collective-permute-start.3 = (f32[24,384]{1,0:T(8,128)S(1)}, f32[24,384]{1,0:T(8,128)S(1)}, u32[]{:S(2)}, u32[]{:S(2)}) collective-permute-start(f32[24,384]{1,0:T(8,128)S(1)} %bitcast_add_fusion), channel_id=1, source_target_pairs={{0,192},{64,0},{128,64},{192,128},{1,193},{65,1},{129,65},{193,129... | collective-permute-start | bytes 110600 | tf_op jit(solution)/shard_map/ppermute | solution.py:206
  12.0 0.3 collective-permute-start.2
  12.3 0.7 %collective-permute-start.1 = (f32[24,384]{1,0:T(8,128)S(1)}, f32[24,384]{1,0:T(8,128)S(1)}, u32[]{:S(2)}, u32[]{:S(2)}) collective-permute-start(f32[24,384]{1,0:T(8,128)S(1)} %bitcast_add_fusion), channel_id=1, source_target_pairs={{0,64},{64,128},{128,192},{192,0},{1,65},{65,129},{129,193},{193,1... | collective-permute-start | bytes 110600 | tf_op jit(solution)/shard_map/ppermute | solution.py:206
  13.0 1.2 %collective-permute-start.9 = (f32[23,32,128]{2,1,0:T(8,128)S(1)}, f32[23,32,128]{2,1,0:T(8,128)S(1)}, u32[]{:S(2)}, u32[]{:S(2)}) collective-permute-start(f32[23,32,128]{2,1,0:T(8,128)S(1)} %get-tuple-element.13), channel_id=1, source_target_pairs={{0,1},{1,2},{2,3},{3,0},{4,5},{5,6},{6,7},{7,4},{8,9},{9,10},{10,1... | collective-permute-start | bytes 1130504 | tf_op jit(solution)/shard_map/ppermute | solution.py:206
  14.2 1.5 %collective-permute-start.10 = (f32[23,32,128]{2,1,0:T(8,128)S(1)}, f32[23,32,128]{2,1,0:T(8,128)S(1)}, u32[]{:S(2)}, u32[]{:S(2)}) collective-permute-start(f32[23,32,128]{2,1,0:T(8,128)S(1)} %get-tuple-element.14), channel_id=1, source_target_pairs={{0,3},{1,0},{2,1},{3,2},{4,7},{5,4},{6,5},{7,6},{8,11},{9,8},{10,9... | collective-permute-start | bytes 1130504 | tf_op jit(solution)/shard_map/ppermute | solution.py:206
  15.7 0.0 collective-permute-done.3
  15.7 0.6 %collective-permute-done.2 = f32[24,384]{1,0:T(8,128)S(1)} collective-permute-done((f32[24,384]{1,0:T(8,128)S(1)}, f32[24,384]{1,0:T(8,128)S(1)}, u32[]{:S(2)}, u32[]{:S(2)}) %collective-permute-start.2) | collective-permute-done | bytes 36896 | tf_op jit(solution)/shard_map/ppermute | solution.py:206
  16.3 0.4 collective-permute-done.1
  16.7 1.7 %collective-permute-start.5 = (f32[24,384]{1,0:T(8,128)S(1)}, f32[24,384]{1,0:T(8,128)S(1)}, u32[]{:S(2)}, u32[]{:S(2)}) collective-permute-start(f32[24,384]{1,0:T(8,128)S(1)} %add_add_fusion.1), channel_id=1, source_target_pairs={{0,8},{8,16},{16,24},{24,32},{32,40},{40,48},{48,56},{56,0},{1,9},... | collective-permute-start | bytes 110600 | tf_op jit(solution)/shard_map/ppermute | solution.py:206
  18.4 4.0 %collective-permute-start.4 = (f32[24,384]{1,0:T(8,128)S(1)}, f32[24,384]{1,0:T(8,128)S(1)}, u32[]{:S(2)}, u32[]{:S(2)}) collective-permute-start(f32[24,384]{1,0:T(8,128)S(1)} %add_add_fusion.1), channel_id=1, source_target_pairs={{0,56},{8,0},{16,8},{24,16},{32,24},{40,32},{48,40},{56,48},{1,57}... | collective-permute-start | bytes 110600 | tf_op jit(solution)/shard_map/ppermute | solution.py:206
  22.4 1.6 %collective-permute-done.5 = f32[24,384]{1,0:T(8,128)S(1)} collective-permute-done((f32[24,384]{1,0:T(8,128)S(1)}, f32[24,384]{1,0:T(8,128)S(1)}, u32[]{:S(2)}, u32[]{:S(2)}) %collective-permute-start.5) | collective-permute-done | bytes 36896 | tf_op jit(solution)/shard_map/ppermute | solution.py:206
  24.0 0.0 collective-permute-done.4
  24.0 4.4 %collective-permute-start.7 = (f32[24,384]{1,0:T(8,128)S(1)}, f32[24,384]{1,0:T(8,128)S(1)}, u32[]{:S(2)}, u32[]{:S(2)}) collective-permute-start(f32[24,384]{1,0:T(8,128)S(1)} %get-tuple-element.20), channel_id=1, source_target_pairs={{0,24},{8,32},{16,40},{24,48},{32,56},{40,0},{48,8},{56,16},{1,25}... | collective-permute-start | bytes 110600 | tf_op jit(solution)/shard_map/ppermute | solution.py:206
  28.4 0.2 collective-permute-start.6
  28.6 0.0 collective-permute-done.9.below_ref
  28.6 0.0 collective-permute-done.10.above_ref
  28.6 0.1 slice_add_fusion
  28.6 1.0 %collective-permute-start.12 = (f32[23,16,128]{2,1,0:T(8,128)S(1)}, f32[23,16,128]{2,1,0:T(8,128)S(1)}, u32[]{:S(2)}, u32[]{:S(2)}) collective-permute-start(f32[23,16,128]{2,1,0:T(8,128)S(1)} %get-tuple-element.21), channel_id=1, source_target_pairs={{0,1},{1,2},{2,3},{3,0},{4,5},{5,6},{6,7},{7,4},{8,9},{9,10},{10,1... | collective-permute-start | bytes 565256 | tf_op jit(solution)/shard_map/ppermute | solution.py:206
  29.6 1.8 %collective-permute-start.11 = (f32[23,16,128]{2,1,0:T(8,128)S(1)}, f32[23,16,128]{2,1,0:T(8,128)S(1)}, u32[]{:S(2)}, u32[]{:S(2)}) collective-permute-start(f32[23,16,128]{2,1,0:T(8,128)S(1)} %get-tuple-element.22), channel_id=1, source_target_pairs={{0,3},{1,0},{2,1},{3,2},{4,7},{5,4},{6,5},{7,6},{8,11},{9,8},{10,9... | collective-permute-start | bytes 565256 | tf_op jit(solution)/shard_map/ppermute | solution.py:206
  31.4 0.0 collective-permute-done.7
  31.4 1.7 %collective-permute-done.6 = f32[24,384]{1,0:T(8,128)S(1)} collective-permute-done((f32[24,384]{1,0:T(8,128)S(1)}, f32[24,384]{1,0:T(8,128)S(1)}, u32[]{:S(2)}, u32[]{:S(2)}) %collective-permute-start.6) | collective-permute-done | bytes 36896 | tf_op jit(solution)/shard_map/ppermute | solution.py:206
  33.1 4.3 %collective-permute-start.8 = (f32[24,384]{1,0:T(8,128)S(1)}, f32[24,384]{1,0:T(8,128)S(1)}, u32[]{:S(2)}, u32[]{:S(2)}) collective-permute-start(f32[24,384]{1,0:T(8,128)S(1)} %add_add_fusion.mine_ref), channel_id=1, source_target_pairs={{0,4},{4,0},{1,5},{5,1},{2,6},{6,2},{3,7},{7,3},{8,12},{12,8},{9,1... | collective-permute-start | bytes 110600 | tf_op jit(solution)/shard_map/ppermute | solution.py:206
  37.4 0.9 %collective-permute-done.8.other_ref = f32[24,384]{1,0:T(8,128)S(1)} collective-permute-done((f32[24,384]{1,0:T(8,128)S(1)}, f32[24,384]{1,0:T(8,128)S(1)}, u32[]{:S(2)}, u32[]{:S(2)}) %collective-permute-start.8) | collective-permute-done | bytes 36896 | tf_op jit(solution)/shard_map/ppermute | solution.py:206
  38.3 0.0 collective-permute-done.12.near_ref
  38.3 0.0 collective-permute-done.11.far_ref
  38.3 1.1 %shard_map.86 = (f32[46,4,92]{2,1,0:T(4,128)}, s32[1,46]{1,0:T(1,128)}, f32[23,4096]{1,0:T(8,128)}) custom-call(f32[24,384]{1,0:T(8,128)S(1)} %add_add_fusion.mine_ref, f32[24,384]{1,0:T(8,128)S(1)} %collective-permute-done.8.other_ref, f32[23,32,128]{2,1,0:T(8,128)S(1)} %get-tuple-element.12.own_ref, f32[23,32,128]{2,1,0:T(8,128)S(1)} %collective-permute-done.9.below_ref, ...), custom_call_target="tpu_custom_call" | custom-call | tf_op jit(solution)/shard_map/pallas_call | solution.py:246
  (5 shorter events, 0.0 us)
Async XLA Ops:
  6.8 4.2 %collective-permute-start = (f32[24,384]{1,0:T(8,128)S(1)}, f32[24,384]{1,0:T(8,128)S(1)}, u32[]{:S(2)}, u32[]{:S(2)}) collective-permute-start(f32[24,384]{1,0:T(8,128)S(1)} %dynamic-slice_bitcast_fusion), channel_id=1, source_target_pairs={{0,4},{4,0},{1,5},{5,1},{2,6},{6,2},{3,7},{7,3},{8,12},{12,8},{9,1... | collective-permute-start | bytes 110600 | tf_op jit(solution)/shard_map/ppermute | solution.py:206
  11.0 4.7 %collective-permute-start.3 = (f32[24,384]{1,0:T(8,128)S(1)}, f32[24,384]{1,0:T(8,128)S(1)}, u32[]{:S(2)}, u32[]{:S(2)}) collective-permute-start(f32[24,384]{1,0:T(8,128)S(1)} %bitcast_add_fusion), channel_id=1, source_target_pairs={{0,192},{64,0},{128,64},{192,128},{1,193},{65,1},{129,65},{193,129... | collective-permute-start | bytes 110600 | tf_op jit(solution)/shard_map/ppermute | solution.py:206
  12.0 4.3 %collective-permute-start.2 = (f32[24,384]{1,0:T(8,128)S(1)}, f32[24,384]{1,0:T(8,128)S(1)}, u32[]{:S(2)}, u32[]{:S(2)}) collective-permute-start(f32[24,384]{1,0:T(8,128)S(1)} %bitcast_add_fusion), channel_id=1, source_target_pairs={{0,128},{64,192},{128,0},{192,64},{1,129},{65,193},{129,1},{193,65... | collective-permute-start | bytes 110600 | tf_op jit(solution)/shard_map/ppermute | solution.py:206
  12.3 4.4 %collective-permute-start.1 = (f32[24,384]{1,0:T(8,128)S(1)}, f32[24,384]{1,0:T(8,128)S(1)}, u32[]{:S(2)}, u32[]{:S(2)}) collective-permute-start(f32[24,384]{1,0:T(8,128)S(1)} %bitcast_add_fusion), channel_id=1, source_target_pairs={{0,64},{64,128},{128,192},{192,0},{1,65},{65,129},{129,193},{193,1... | collective-permute-start | bytes 110600 | tf_op jit(solution)/shard_map/ppermute | solution.py:206
  13.0 15.6 %collective-permute-start.9 = (f32[23,32,128]{2,1,0:T(8,128)S(1)}, f32[23,32,128]{2,1,0:T(8,128)S(1)}, u32[]{:S(2)}, u32[]{:S(2)}) collective-permute-start(f32[23,32,128]{2,1,0:T(8,128)S(1)} %get-tuple-element.13), channel_id=1, source_target_pairs={{0,1},{1,2},{2,3},{3,0},{4,5},{5,6},{6,7},{7,4},{8,9},{9,10},{10,1... | collective-permute-start | bytes 1130504 | tf_op jit(solution)/shard_map/ppermute | solution.py:206
  14.2 14.3 %collective-permute-start.10 = (f32[23,32,128]{2,1,0:T(8,128)S(1)}, f32[23,32,128]{2,1,0:T(8,128)S(1)}, u32[]{:S(2)}, u32[]{:S(2)}) collective-permute-start(f32[23,32,128]{2,1,0:T(8,128)S(1)} %get-tuple-element.14), channel_id=1, source_target_pairs={{0,3},{1,0},{2,1},{3,2},{4,7},{5,4},{6,5},{7,6},{8,11},{9,8},{10,9... | collective-permute-start | bytes 1130504 | tf_op jit(solution)/shard_map/ppermute | solution.py:206
  16.7 7.3 %collective-permute-start.5 = (f32[24,384]{1,0:T(8,128)S(1)}, f32[24,384]{1,0:T(8,128)S(1)}, u32[]{:S(2)}, u32[]{:S(2)}) collective-permute-start(f32[24,384]{1,0:T(8,128)S(1)} %add_add_fusion.1), channel_id=1, source_target_pairs={{0,8},{8,16},{16,24},{24,32},{32,40},{40,48},{48,56},{56,0},{1,9},... | collective-permute-start | bytes 110600 | tf_op jit(solution)/shard_map/ppermute | solution.py:206
  18.4 5.6 %collective-permute-start.4 = (f32[24,384]{1,0:T(8,128)S(1)}, f32[24,384]{1,0:T(8,128)S(1)}, u32[]{:S(2)}, u32[]{:S(2)}) collective-permute-start(f32[24,384]{1,0:T(8,128)S(1)} %add_add_fusion.1), channel_id=1, source_target_pairs={{0,56},{8,0},{16,8},{24,16},{32,24},{40,32},{48,40},{56,48},{1,57}... | collective-permute-start | bytes 110600 | tf_op jit(solution)/shard_map/ppermute | solution.py:206
  24.0 7.4 %collective-permute-start.7 = (f32[24,384]{1,0:T(8,128)S(1)}, f32[24,384]{1,0:T(8,128)S(1)}, u32[]{:S(2)}, u32[]{:S(2)}) collective-permute-start(f32[24,384]{1,0:T(8,128)S(1)} %get-tuple-element.20), channel_id=1, source_target_pairs={{0,24},{8,32},{16,40},{24,48},{32,56},{40,0},{48,8},{56,16},{1,25}... | collective-permute-start | bytes 110600 | tf_op jit(solution)/shard_map/ppermute | solution.py:206
  28.4 4.7 %collective-permute-start.6 = (f32[24,384]{1,0:T(8,128)S(1)}, f32[24,384]{1,0:T(8,128)S(1)}, u32[]{:S(2)}, u32[]{:S(2)}) collective-permute-start(f32[24,384]{1,0:T(8,128)S(1)} %get-tuple-element.19), channel_id=1, source_target_pairs={{0,40},{8,48},{16,56},{24,0},{32,8},{40,16},{48,24},{56,32},{1,41}... | collective-permute-start | bytes 110600 | tf_op jit(solution)/shard_map/ppermute | solution.py:206
  28.6 9.7 %collective-permute-start.12 = (f32[23,16,128]{2,1,0:T(8,128)S(1)}, f32[23,16,128]{2,1,0:T(8,128)S(1)}, u32[]{:S(2)}, u32[]{:S(2)}) collective-permute-start(f32[23,16,128]{2,1,0:T(8,128)S(1)} %get-tuple-element.21), channel_id=1, source_target_pairs={{0,1},{1,2},{2,3},{3,0},{4,5},{5,6},{6,7},{7,4},{8,9},{9,10},{10,1... | collective-permute-start | bytes 565256 | tf_op jit(solution)/shard_map/ppermute | solution.py:206
  29.6 8.7 %collective-permute-start.11 = (f32[23,16,128]{2,1,0:T(8,128)S(1)}, f32[23,16,128]{2,1,0:T(8,128)S(1)}, u32[]{:S(2)}, u32[]{:S(2)}) collective-permute-start(f32[23,16,128]{2,1,0:T(8,128)S(1)} %get-tuple-element.22), channel_id=1, source_target_pairs={{0,3},{1,0},{2,1},{3,2},{4,7},{5,4},{6,5},{7,6},{8,11},{9,8},{10,9... | collective-permute-start | bytes 565256 | tf_op jit(solution)/shard_map/ppermute | solution.py:206
  33.1 5.2 %collective-permute-start.8 = (f32[24,384]{1,0:T(8,128)S(1)}, f32[24,384]{1,0:T(8,128)S(1)}, u32[]{:S(2)}, u32[]{:S(2)}) collective-permute-start(f32[24,384]{1,0:T(8,128)S(1)} %add_add_fusion.mine_ref), channel_id=1, source_target_pairs={{0,4},{4,0},{1,5},{5,1},{2,6},{6,2},{3,7},{7,3},{8,12},{12,8},{9,1... | collective-permute-start | bytes 110600 | tf_op jit(solution)/shard_map/ppermute | solution.py:206

commit v6 on v5

--- a/solution.py
+++ b/solution.py
@@ -212,7 +212,7 @@
     mine = lax.dynamic_index_in_dim(halves, core, 0, False)
     other = lax.dynamic_index_in_dim(halves, 1 - core, 0, False)
     mine = mine + moved(other, "core", 1)
-    mine = mine + moved(mine, "y", 1) + moved(mine, "y", 2) + moved(mine, "y", 3)
+    mine = mine + moved(mine, "y", 1) + moved(mine, "y", 3) + moved(mine, "y", 2)
     two = mine + moved(mine, "z", 7)
     three = two + moved(mine, "z", 1)
     mine = three + moved(three, "z", 5) + moved(two, "z", 3)

time: 39.5 us -> 40 us (1.013)
  starting transfers between devices: 25.4 us -> 26.1 us
    ppermute x13, starting transfers between devices: 25.4 us -> 26.1 us  [moved(): lax.ppermute(array, axis, [(i, (i + shift) % size) for i in range(size)])]
  transfers between devices with their start and end apart: 13 -> 13, of which waited for: 6 -> 5; matrix products, arithmetic and copies ran while one was open for 0% -> 0% of each run, Pallas kernels for 0% -> 0%
where the time goes in v6:
time: 40 us; the launch traced here: 39.9 us
  starting transfers between devices  26.1 us (65%)
  Pallas kernels  7.22 us (18%)
  waiting for transfers between devices  5.84 us (15%)
  between operations  0.68 us (2%)
    ppermute x13, starting transfers between devices, moved(): lax.ppermute(array, axis, [(i, (i + shift) % size) for i in range(size)])  26.1 us
    pallas_call x1, Pallas kernels, call(): pl.pallas_call(kernel, grid=(tiles // TILES,), in_specs=[pl.BlockSpec(fil...  6.11 us
    ppermute x13, waiting for transfers between devices, moved(): lax.ppermute(array, axis, [(i, (i + shift) % size) for i in range(size)])  5.84 us
    pallas_call x1, Pallas kernels, shards(): pl.pallas_call(last_kernel, out_shape=[jax.ShapeDtypeStruct((REGIONS, mem...  1.11 us
  transfers between devices with their start and end apart: 13, of which 5 were waited for; matrix products, arithmetic and copies ran while one was open for 0% of the time, Pallas kernels for 0%

profile of v6, /device:TPU:1, one launch (start us, length us, event | category | flops | bytes accessed | tf_op | source)
XLA Modules:
  0.0 39.9 jit_solution(3309405044955633411)
XLA Ops:
  0.6 6.1 %shard_map.85 = (f32[23,32,128]{2,1,0:T(8,128)S(1)}, f32[23,32,128]{2,1,0:T(8,128)S(1)}, f32[23,32,128]{2,1,0:T(8,128)S(1)}, f32[23,32,128]{2,1,0:T(8,128)S(1)}, f32[48,384]{1,0:T(8,128)S(1)}) custom-call(s32[1,32]{1,0:T(1,128)} %bitcast.24, f32[97,128,128]{2,1,0:T(8,128)} %bitcast.19, s32[32,128]{1,0:T(8,128)} %bitcast.20, s32[32,128]{1,0:T(8,128)} %bitcast.21, ...), custom_call_target="tpu_custom_call" | custom-call | tf_op jit(solution)/shard_map/pallas_call | solution.py:189
  6.8 3.3 %collective-permute-start = (f32[24,384]{1,0:T(8,128)S(1)}, f32[24,384]{1,0:T(8,128)S(1)}, u32[]{:S(2)}, u32[]{:S(2)}) collective-permute-start(f32[24,384]{1,0:T(8,128)S(1)} %dynamic-slice_bitcast_fusion), channel_id=1, source_target_pairs={{0,4},{4,0},{1,5},{5,1},{2,6},{6,2},{3,7},{7,3},{8,12},{12,8},{9,1... | collective-permute-start | bytes 110600 | tf_op jit(solution)/shard_map/ppermute | solution.py:206
  10.1 0.9 %collective-permute-done = f32[24,384]{1,0:T(8,128)S(1)} collective-permute-done((f32[24,384]{1,0:T(8,128)S(1)}, f32[24,384]{1,0:T(8,128)S(1)}, u32[]{:S(2)}, u32[]{:S(2)}) %collective-permute-start) | collective-permute-done | bytes 36896 | tf_op jit(solution)/shard_map/ppermute | solution.py:206
  11.0 1.2 %collective-permute-start.3 = (f32[24,384]{1,0:T(8,128)S(1)}, f32[24,384]{1,0:T(8,128)S(1)}, u32[]{:S(2)}, u32[]{:S(2)}) collective-permute-start(f32[24,384]{1,0:T(8,128)S(1)} %bitcast_add_fusion), channel_id=1, source_target_pairs={{0,128},{64,192},{128,0},{192,64},{1,129},{65,193},{129,1},{193,65... | collective-permute-start | bytes 110600 | tf_op jit(solution)/shard_map/ppermute | solution.py:206
  12.1 0.8 %collective-permute-start.2 = (f32[24,384]{1,0:T(8,128)S(1)}, f32[24,384]{1,0:T(8,128)S(1)}, u32[]{:S(2)}, u32[]{:S(2)}) collective-permute-start(f32[24,384]{1,0:T(8,128)S(1)} %bitcast_add_fusion), channel_id=1, source_target_pairs={{0,192},{64,0},{128,64},{192,128},{1,193},{65,1},{129,65},{193,129... | collective-permute-start | bytes 110600 | tf_op jit(solution)/shard_map/ppermute | solution.py:206
  12.9 0.7 %collective-permute-start.1 = (f32[24,384]{1,0:T(8,128)S(1)}, f32[24,384]{1,0:T(8,128)S(1)}, u32[]{:S(2)}, u32[]{:S(2)}) collective-permute-start(f32[24,384]{1,0:T(8,128)S(1)} %bitcast_add_fusion), channel_id=1, source_target_pairs={{0,64},{64,128},{128,192},{192,0},{1,65},{65,129},{129,193},{193,1... | collective-permute-start | bytes 110600 | tf_op jit(solution)/shard_map/ppermute | solution.py:206
  13.6 1.2 %collective-permute-start.9 = (f32[23,32,128]{2,1,0:T(8,128)S(1)}, f32[23,32,128]{2,1,0:T(8,128)S(1)}, u32[]{:S(2)}, u32[]{:S(2)}) collective-permute-start(f32[23,32,128]{2,1,0:T(8,128)S(1)} %get-tuple-element.13), channel_id=1, source_target_pairs={{0,1},{1,2},{2,3},{3,0},{4,5},{5,6},{6,7},{7,4},{8,9},{9,10},{10,1... | collective-permute-start | bytes 1130504 | tf_op jit(solution)/shard_map/ppermute | solution.py:206
  14.8 1.5 %collective-permute-start.10 = (f32[23,32,128]{2,1,0:T(8,128)S(1)}, f32[23,32,128]{2,1,0:T(8,128)S(1)}, u32[]{:S(2)}, u32[]{:S(2)}) collective-permute-start(f32[23,32,128]{2,1,0:T(8,128)S(1)} %get-tuple-element.14), channel_id=1, source_target_pairs={{0,3},{1,0},{2,1},{3,2},{4,7},{5,4},{6,5},{7,6},{8,11},{9,8},{10,9... | collective-permute-start | bytes 1130504 | tf_op jit(solution)/shard_map/ppermute | solution.py:206
  16.3 0.0 collective-permute-done.3
  16.3 0.0 collective-permute-done.2
  16.3 0.6 %collective-permute-done.1 = f32[24,384]{1,0:T(8,128)S(1)} collective-permute-done((f32[24,384]{1,0:T(8,128)S(1)}, f32[24,384]{1,0:T(8,128)S(1)}, u32[]{:S(2)}, u32[]{:S(2)}) %collective-permute-start.1) | collective-permute-done | bytes 36896 | tf_op jit(solution)/shard_map/ppermute | solution.py:206
  17.0 1.7 %collective-permute-start.5 = (f32[24,384]{1,0:T(8,128)S(1)}, f32[24,384]{1,0:T(8,128)S(1)}, u32[]{:S(2)}, u32[]{:S(2)}) collective-permute-start(f32[24,384]{1,0:T(8,128)S(1)} %add_add_fusion.1), channel_id=1, source_target_pairs={{0,8},{8,16},{16,24},{24,32},{32,40},{40,48},{48,56},{56,0},{1,9},... | collective-permute-start | bytes 110600 | tf_op jit(solution)/shard_map/ppermute | solution.py:206
  18.7 4.0 %collective-permute-start.4 = (f32[24,384]{1,0:T(8,128)S(1)}, f32[24,384]{1,0:T(8,128)S(1)}, u32[]{:S(2)}, u32[]{:S(2)}) collective-permute-start(f32[24,384]{1,0:T(8,128)S(1)} %add_add_fusion.1), channel_id=1, source_target_pairs={{0,56},{8,0},{16,8},{24,16},{32,24},{40,32},{48,40},{56,48},{1,57}... | collective-permute-start | bytes 110600 | tf_op jit(solution)/shard_map/ppermute | solution.py:206
  22.7 1.6 %collective-permute-done.5 = f32[24,384]{1,0:T(8,128)S(1)} collective-permute-done((f32[24,384]{1,0:T(8,128)S(1)}, f32[24,384]{1,0:T(8,128)S(1)}, u32[]{:S(2)}, u32[]{:S(2)}) %collective-permute-start.5) | collective-permute-done | bytes 36896 | tf_op jit(solution)/shard_map/ppermute | solution.py:206
  24.3 0.0 collective-permute-done.4
  24.3 4.4 %collective-permute-start.7 = (f32[24,384]{1,0:T(8,128)S(1)}, f32[24,384]{1,0:T(8,128)S(1)}, u32[]{:S(2)}, u32[]{:S(2)}) collective-permute-start(f32[24,384]{1,0:T(8,128)S(1)} %get-tuple-element.20), channel_id=1, source_target_pairs={{0,24},{8,32},{16,40},{24,48},{32,56},{40,0},{48,8},{56,16},{1,25}... | collective-permute-start | bytes 110600 | tf_op jit(solution)/shard_map/ppermute | solution.py:206
  28.6 0.2 collective-permute-start.6
  28.8 0.0 collective-permute-done.9.below_ref
  28.8 0.0 collective-permute-done.10.above_ref
  28.8 0.1 slice_add_fusion
  28.9 1.0 %collective-permute-start.12 = (f32[23,16,128]{2,1,0:T(8,128)S(1)}, f32[23,16,128]{2,1,0:T(8,128)S(1)}, u32[]{:S(2)}, u32[]{:S(2)}) collective-permute-start(f32[23,16,128]{2,1,0:T(8,128)S(1)} %get-tuple-element.21), channel_id=1, source_target_pairs={{0,1},{1,2},{2,3},{3,0},{4,5},{5,6},{6,7},{7,4},{8,9},{9,10},{10,1... | collective-permute-start | bytes 565256 | tf_op jit(solution)/shard_map/ppermute | solution.py:206
  29.9 1.8 %collective-permute-start.11 = (f32[23,16,128]{2,1,0:T(8,128)S(1)}, f32[23,16,128]{2,1,0:T(8,128)S(1)}, u32[]{:S(2)}, u32[]{:S(2)}) collective-permute-start(f32[23,16,128]{2,1,0:T(8,128)S(1)} %get-tuple-element.22), channel_id=1, source_target_pairs={{0,3},{1,0},{2,1},{3,2},{4,7},{5,4},{6,5},{7,6},{8,11},{9,8},{10,9... | collective-permute-start | bytes 565256 | tf_op jit(solution)/shard_map/ppermute | solution.py:206
  31.6 0.0 collective-permute-done.7
  31.6 1.9 %collective-permute-done.6 = f32[24,384]{1,0:T(8,128)S(1)} collective-permute-done((f32[24,384]{1,0:T(8,128)S(1)}, f32[24,384]{1,0:T(8,128)S(1)}, u32[]{:S(2)}, u32[]{:S(2)}) %collective-permute-start.6) | collective-permute-done | bytes 36896 | tf_op jit(solution)/shard_map/ppermute | solution.py:206
  33.5 4.4 %collective-permute-start.8 = (f32[24,384]{1,0:T(8,128)S(1)}, f32[24,384]{1,0:T(8,128)S(1)}, u32[]{:S(2)}, u32[]{:S(2)}) collective-permute-start(f32[24,384]{1,0:T(8,128)S(1)} %add_add_fusion.mine_ref), channel_id=1, source_target_pairs={{0,4},{4,0},{1,5},{5,1},{2,6},{6,2},{3,7},{7,3},{8,12},{12,8},{9,1... | collective-permute-start | bytes 110600 | tf_op jit(solution)/shard_map/ppermute | solution.py:206
  38.0 0.9 %collective-permute-done.8.other_ref = f32[24,384]{1,0:T(8,128)S(1)} collective-permute-done((f32[24,384]{1,0:T(8,128)S(1)}, f32[24,384]{1,0:T(8,128)S(1)}, u32[]{:S(2)}, u32[]{:S(2)}) %collective-permute-start.8) | collective-permute-done | bytes 36896 | tf_op jit(solution)/shard_map/ppermute | solution.py:206
  38.8 0.0 collective-permute-done.12.near_ref
  38.8 0.0 collective-permute-done.11.far_ref
  38.8 1.1 %shard_map.86 = (f32[46,4,92]{2,1,0:T(4,128)}, s32[1,46]{1,0:T(1,128)}, f32[23,4096]{1,0:T(8,128)}) custom-call(f32[24,384]{1,0:T(8,128)S(1)} %add_add_fusion.mine_ref, f32[24,384]{1,0:T(8,128)S(1)} %collective-permute-done.8.other_ref, f32[23,32,128]{2,1,0:T(8,128)S(1)} %get-tuple-element.12.own_ref, f32[23,32,128]{2,1,0:T(8,128)S(1)} %collective-permute-done.9.below_ref, ...), custom_call_target="tpu_custom_call" | custom-call | tf_op jit(solution)/shard_map/pallas_call | solution.py:246
  (5 shorter events, 0.0 us)
Async XLA Ops:
  6.8 4.2 %collective-permute-start = (f32[24,384]{1,0:T(8,128)S(1)}, f32[24,384]{1,0:T(8,128)S(1)}, u32[]{:S(2)}, u32[]{:S(2)}) collective-permute-start(f32[24,384]{1,0:T(8,128)S(1)} %dynamic-slice_bitcast_fusion), channel_id=1, source_target_pairs={{0,4},{4,0},{1,5},{5,1},{2,6},{6,2},{3,7},{7,3},{8,12},{12,8},{9,1... | collective-permute-start | bytes 110600 | tf_op jit(solution)/shard_map/ppermute | solution.py:206
  11.0 5.3 %collective-permute-start.3 = (f32[24,384]{1,0:T(8,128)S(1)}, f32[24,384]{1,0:T(8,128)S(1)}, u32[]{:S(2)}, u32[]{:S(2)}) collective-permute-start(f32[24,384]{1,0:T(8,128)S(1)} %bitcast_add_fusion), channel_id=1, source_target_pairs={{0,128},{64,192},{128,0},{192,64},{1,129},{65,193},{129,1},{193,65... | collective-permute-start | bytes 110600 | tf_op jit(solution)/shard_map/ppermute | solution.py:206
  12.1 4.2 %collective-permute-start.2 = (f32[24,384]{1,0:T(8,128)S(1)}, f32[24,384]{1,0:T(8,128)S(1)}, u32[]{:S(2)}, u32[]{:S(2)}) collective-permute-start(f32[24,384]{1,0:T(8,128)S(1)} %bitcast_add_fusion), channel_id=1, source_target_pairs={{0,192},{64,0},{128,64},{192,128},{1,193},{65,1},{129,65},{193,129... | collective-permute-start | bytes 110600 | tf_op jit(solution)/shard_map/ppermute | solution.py:206
  12.9 4.0 %collective-permute-start.1 = (f32[24,384]{1,0:T(8,128)S(1)}, f32[24,384]{1,0:T(8,128)S(1)}, u32[]{:S(2)}, u32[]{:S(2)}) collective-permute-start(f32[24,384]{1,0:T(8,128)S(1)} %bitcast_add_fusion), channel_id=1, source_target_pairs={{0,64},{64,128},{128,192},{192,0},{1,65},{65,129},{129,193},{193,1... | collective-permute-start | bytes 110600 | tf_op jit(solution)/shard_map/ppermute | solution.py:206
  13.6 15.2 %collective-permute-start.9 = (f32[23,32,128]{2,1,0:T(8,128)S(1)}, f32[23,32,128]{2,1,0:T(8,128)S(1)}, u32[]{:S(2)}, u32[]{:S(2)}) collective-permute-start(f32[23,32,128]{2,1,0:T(8,128)S(1)} %get-tuple-element.13), channel_id=1, source_target_pairs={{0,1},{1,2},{2,3},{3,0},{4,5},{5,6},{6,7},{7,4},{8,9},{9,10},{10,1... | collective-permute-start | bytes 1130504 | tf_op jit(solution)/shard_map/ppermute | solution.py:206
  14.8 14.0 %collective-permute-start.10 = (f32[23,32,128]{2,1,0:T(8,128)S(1)}, f32[23,32,128]{2,1,0:T(8,128)S(1)}, u32[]{:S(2)}, u32[]{:S(2)}) collective-permute-start(f32[23,32,128]{2,1,0:T(8,128)S(1)} %get-tuple-element.14), channel_id=1, source_target_pairs={{0,3},{1,0},{2,1},{3,2},{4,7},{5,4},{6,5},{7,6},{8,11},{9,8},{10,9... | collective-permute-start | bytes 1130504 | tf_op jit(solution)/shard_map/ppermute | solution.py:206
  17.0 7.3 %collective-permute-start.5 = (f32[24,384]{1,0:T(8,128)S(1)}, f32[24,384]{1,0:T(8,128)S(1)}, u32[]{:S(2)}, u32[]{:S(2)}) collective-permute-start(f32[24,384]{1,0:T(8,128)S(1)} %add_add_fusion.1), channel_id=1, source_target_pairs={{0,8},{8,16},{16,24},{24,32},{32,40},{40,48},{48,56},{56,0},{1,9},... | collective-permute-start | bytes 110600 | tf_op jit(solution)/shard_map/ppermute | solution.py:206
  18.7 5.6 %collective-permute-start.4 = (f32[24,384]{1,0:T(8,128)S(1)}, f32[24,384]{1,0:T(8,128)S(1)}, u32[]{:S(2)}, u32[]{:S(2)}) collective-permute-start(f32[24,384]{1,0:T(8,128)S(1)} %add_add_fusion.1), channel_id=1, source_target_pairs={{0,56},{8,0},{16,8},{24,16},{32,24},{40,32},{48,40},{56,48},{1,57}... | collective-permute-start | bytes 110600 | tf_op jit(solution)/shard_map/ppermute | solution.py:206
  24.3 7.4 %collective-permute-start.7 = (f32[24,384]{1,0:T(8,128)S(1)}, f32[24,384]{1,0:T(8,128)S(1)}, u32[]{:S(2)}, u32[]{:S(2)}) collective-permute-start(f32[24,384]{1,0:T(8,128)S(1)} %get-tuple-element.20), channel_id=1, source_target_pairs={{0,24},{8,32},{16,40},{24,48},{32,56},{40,0},{48,8},{56,16},{1,25}... | collective-permute-start | bytes 110600 | tf_op jit(solution)/shard_map/ppermute | solution.py:206
  28.6 4.9 %collective-permute-start.6 = (f32[24,384]{1,0:T(8,128)S(1)}, f32[24,384]{1,0:T(8,128)S(1)}, u32[]{:S(2)}, u32[]{:S(2)}) collective-permute-start(f32[24,384]{1,0:T(8,128)S(1)} %get-tuple-element.19), channel_id=1, source_target_pairs={{0,40},{8,48},{16,56},{24,0},{32,8},{40,16},{48,24},{56,32},{1,41}... | collective-permute-start | bytes 110600 | tf_op jit(solution)/shard_map/ppermute | solution.py:206
  28.9 9.9 %collective-permute-start.12 = (f32[23,16,128]{2,1,0:T(8,128)S(1)}, f32[23,16,128]{2,1,0:T(8,128)S(1)}, u32[]{:S(2)}, u32[]{:S(2)}) collective-permute-start(f32[23,16,128]{2,1,0:T(8,128)S(1)} %get-tuple-element.21), channel_id=1, source_target_pairs={{0,1},{1,2},{2,3},{3,0},{4,5},{5,6},{6,7},{7,4},{8,9},{9,10},{10,1... | collective-permute-start | bytes 565256 | tf_op jit(solution)/shard_map/ppermute | solution.py:206
  29.9 9.0 %collective-permute-start.11 = (f32[23,16,128]{2,1,0:T(8,128)S(1)}, f32[23,16,128]{2,1,0:T(8,128)S(1)}, u32[]{:S(2)}, u32[]{:S(2)}) collective-permute-start(f32[23,16,128]{2,1,0:T(8,128)S(1)} %get-tuple-element.22), channel_id=1, source_target_pairs={{0,3},{1,0},{2,1},{3,2},{4,7},{5,4},{6,5},{7,6},{8,11},{9,8},{10,9... | collective-permute-start | bytes 565256 | tf_op jit(solution)/shard_map/ppermute | solution.py:206
  33.5 5.3 %collective-permute-start.8 = (f32[24,384]{1,0:T(8,128)S(1)}, f32[24,384]{1,0:T(8,128)S(1)}, u32[]{:S(2)}, u32[]{:S(2)}) collective-permute-start(f32[24,384]{1,0:T(8,128)S(1)} %add_add_fusion.mine_ref), channel_id=1, source_target_pairs={{0,4},{4,0},{1,5},{5,1},{2,6},{6,2},{3,7},{7,3},{8,12},{12,8},{9,1... | collective-permute-start | bytes 110600 | tf_op jit(solution)/shard_map/ppermute | solution.py:206
